TPU v7x, 512 devices: a whole 4x4x16 slice. The times are simulated.
512 devices in a mesh: row: 32 (over z, y_lo), col: 16 (over y_hi, x, core).
Axes of the slice: x: 4, y: 4 (y_hi: 2, y_lo: 2; y = y_hi * 2 + y_lo), z: 16, core: 2. Of those that a mesh axis runs over, the one named last changes fastest.
Arguments:
- atom_feats: bfloat16 [32768, 128], P(('row', 'col')), may hold values from -6 to 6
- key_starts: int32 [1024], P(('row', 'col')), may hold values from -64 to 32704, as said below
- atom_counts: int32 [2048], replicated, may hold values from 8 to 24, as said below
- atom_gain: float32 [128], replicated, may hold values from 0.1 to 1.9
- w_query: bfloat16 [128, 128], replicated, may hold values from -0.5 to 0.5
- w_key: bfloat16 [128, 128], replicated, may hold values from -0.5 to 0.5
- w_value: bfloat16 [128, 128], replicated, may hold values from -0.5 to 0.5
- w_out: bfloat16 [128, 128], replicated, may hold values from -0.5 to 0.5
- w_pool: bfloat16 [128, 384], replicated, may hold values from -0.5 to 0.5
- w_back: bfloat16 [384, 128], replicated, may hold values from -0.3125 to 0.3125
- pair_state: bfloat16 [2048, 2048, 128], P('row', 'col'), may hold values from -6 to 6
- w_left: bfloat16 [384, 32], replicated, may hold values from -0.3125 to 0.3125
- w_right: bfloat16 [384, 32], replicated, may hold values from -0.3125 to 0.3125
- w_outer: bfloat16 [32, 32, 128], replicated, may hold values from -0.1875 to 0.1875
- pair_gain: float32 [128], replicated, may hold values from 0.1 to 1.9
- w_gate: bfloat16 [128, 512], replicated, may hold values from -0.5 to 0.5
- w_lift: bfloat16 [128, 512], replicated, may hold values from -0.5 to 0.5
- w_drop: bfloat16 [512, 128], replicated, may hold values from -0.25 to 0.25
Outputs:
- atom_out: bfloat16 [32768, 128], P(('row', 'col'))
- token_single: bfloat16 [2048, 384], P(('row', 'col'))
- pair_out: bfloat16 [2048, 2048, 128], P('row', 'col')
Inputs may be any that keep to these rules, and one draw needn't show every extreme that they name: key_starts[b] = 32 * b - 64 + offset, with offset a whole number from 0 to 32; the offset is 0 for the first block and 32 for the last. `atom_counts`: the counts sum to 32768.
All inputs are finite; a program needn't handle non-finite values.
Results may differ from a plain program's by a relative error of at most 0.007.
Values may be sent and summed in bfloat16 or wider, within the bound.
A program may use at most 64 MiB of HBM per device.

v0:
```python
import math

import jax
import jax.numpy as jnp
from jax import lax
from jax.sharding import PartitionSpec as P

HEADS = 4
QB = 32
KW = 128
FEWEST = 8


EPSILON = 1e-05


def with_halo(block, sides, width):
    for axis, dim in sides:
        count = lax.axis_size(axis)
        forward = [(i, i + 1) for i in range(count - 1)]
        backward = [(target, source) for source, target in forward]
        low = lax.ppermute(
            lax.slice_in_dim(block, block.shape[dim] - width, None, axis=dim), axis, forward
        )
        high = lax.ppermute(lax.slice_in_dim(block, 0, width, axis=dim), axis, backward)
        block = jnp.concatenate([low, block, high], axis=dim)
    return block


def shifted(block, axis, distance):
    devices = range(lax.axis_size(axis))
    route = [(i - distance, i) for i in devices if i - distance in devices]
    return lax.ppermute(block, axis, route)


def layer_norm(values, gain):
    mean_value = jnp.mean(values, axis=-1, keepdims=True)
    centred = values - mean_value
    variance = jnp.mean(centred * centred, axis=-1, keepdims=True)
    return centred * lax.rsqrt(variance + EPSILON) * gain


def project(source, weight):
    return jnp.dot(source, weight, preferred_element_type=jnp.float32).astype(jnp.bfloat16)


def per_device(
    atom_feats,
    key_starts,
    atom_counts,
    atom_gain,
    w_query,
    w_key,
    w_value,
    w_out,
    w_pool,
    w_back,
    pair_state,
    w_left,
    w_right,
    w_outer,
    pair_gain,
    w_gate,
    w_lift,
    w_drop,
):
    atom_rows, atom_width = atom_feats.shape
    devices = lax.axis_size(("row", "col"))
    position = lax.axis_index(("row", "col"))
    total_atoms = atom_rows * devices
    total_tokens = atom_counts.shape[0]
    own_tokens = total_tokens // devices
    rim_width = KW // 2
    first_atom = position * atom_rows
    atom_float = atom_feats.astype(jnp.float32)
    normed = layer_norm(atom_float, atom_gain).astype(jnp.bfloat16)
    queries = project(normed, w_query)
    w_keyval = jnp.concatenate([w_key, w_value], axis=1)
    keyvals = project(normed, w_keyval)
    extended = with_halo(keyvals, ((("row", "col"), 0),), rim_width)
    local_starts = key_starts - first_atom + rim_width
    windows = jax.vmap(lambda first_row: lax.dynamic_slice_in_dim(extended, first_row, KW, 0))(
        local_starts
    )
    head_size = atom_width // HEADS
    blocks = atom_rows // QB
    query_blocks = queries.reshape(blocks, QB, HEADS, head_size)
    key_blocks = windows[:, :, :atom_width].reshape(blocks, KW, HEADS, head_size)
    value_blocks = windows[:, :, atom_width:].reshape(blocks, KW, HEADS, head_size)
    key_index = key_starts[:, None] + jnp.arange(KW, dtype=jnp.int32)[None, :]
    in_range = (key_index >= 0) & (key_index < total_atoms)
    scores = jnp.einsum(
        "bqhd,bkhd->bhqk", query_blocks, key_blocks, preferred_element_type=jnp.float32
    ) * head_size ** (-0.5)
    raised = jnp.where(in_range[:, None, None, :], jnp.exp(scores), 0.0)
    weights = (raised / jnp.sum(raised, axis=-1, keepdims=True)).astype(jnp.bfloat16)
    attended = (
        jnp.einsum("bhqk,bkhd->bqhd", weights, value_blocks, preferred_element_type=jnp.float32)
        .astype(jnp.bfloat16)
        .reshape(atom_rows, atom_width)
    )
    updated = (atom_float + jnp.dot(attended, w_out, preferred_element_type=jnp.float32)).astype(
        jnp.bfloat16
    )
    feature = jax.nn.relu(jnp.dot(updated, w_pool, preferred_element_type=jnp.float32)).astype(
        jnp.bfloat16
    )
    token_ends = jnp.cumsum(atom_counts, dtype=jnp.int32)
    atom_index = first_atom + jnp.arange(atom_rows, dtype=jnp.int32)
    token_of = jnp.sum((token_ends[None, :] <= atom_index[:, None]).astype(jnp.int32), axis=1)
    count_float = atom_counts.astype(jnp.float32)
    slots = atom_rows // FEWEST
    token_starts = token_ends - atom_counts
    base_token = jnp.sum((token_starts < first_atom).astype(jnp.int32))
    relative = token_of - base_token
    slot_range = jnp.arange(slots, dtype=jnp.int32)
    member = (relative[:, None] == slot_range[None, :]).astype(jnp.bfloat16)
    local_sums = jnp.einsum("as,ac->sc", member, feature, preferred_element_type=jnp.float32)
    carried = (relative < 0).astype(jnp.bfloat16)[None, :]
    edge_sum = jnp.dot(carried, feature, preferred_element_type=jnp.float32)
    from_next = shifted(edge_sum, ("row", "col"), -1)
    next_token = jnp.sum((token_ends <= first_atom + atom_rows).astype(jnp.int32))
    target = (slot_range == next_token - base_token).astype(jnp.float32)[:, None]
    pooled_slots = local_sums + target * from_next
    padded_counts = jnp.concatenate([count_float, jnp.ones((slots,), jnp.float32)])
    slot_counts = lax.dynamic_slice_in_dim(padded_counts, base_token, slots, 0)
    slot_single = (pooled_slots / slot_counts[:, None]).astype(jnp.bfloat16)
    owner = token_starts // atom_rows
    owner_first = jnp.searchsorted(token_starts, owner * atom_rows, side="left")
    row_of = owner * slots + jnp.arange(total_tokens, dtype=jnp.int32) - owner_first
    gathered = lax.all_gather(slot_single, ("row", "col"), axis=0, tiled=True)
    full_single = jnp.take(gathered, row_of, axis=0)
    left_all = project(full_single, w_left)
    right_all = project(full_single, w_right)
    back_all = project(full_single, w_back)
    token_single = lax.dynamic_slice_in_dim(full_single, position * own_tokens, own_tokens, 0)
    member_all = (token_of[:, None] == jnp.arange(total_tokens, dtype=jnp.int32)[None, :]).astype(
        jnp.bfloat16
    )
    lifted = jnp.dot(member_all, back_all, preferred_element_type=jnp.float32)
    atom_out = (updated.astype(jnp.float32) + lifted).astype(jnp.bfloat16)
    row_tokens, col_tokens, pair_width = pair_state.shape
    left_rows = lax.dynamic_slice_in_dim(
        left_all, lax.axis_index("row") * row_tokens, row_tokens, 0
    )
    right_cols = lax.dynamic_slice_in_dim(
        right_all, lax.axis_index("col") * col_tokens, col_tokens, 0
    )
    outer_table = jnp.einsum(
        "jb,abc->jac", right_cols, w_outer, preferred_element_type=jnp.float32
    ).astype(jnp.bfloat16)
    step_rows = math.gcd(row_tokens, 8)

    def pair_block(pieces):
        left_block, pair_piece = pieces
        outer_term = jnp.einsum(
            "ia,jac->ijc", left_block, outer_table, preferred_element_type=jnp.float32
        )
        summed = pair_piece.astype(jnp.float32) + outer_term
        normed_pair = layer_norm(summed, pair_gain).astype(jnp.bfloat16)
        gate_proj = jnp.einsum(
            "ijc,cf->ijf", normed_pair, w_gate, preferred_element_type=jnp.float32
        )
        lift_proj = jnp.einsum(
            "ijc,cf->ijf", normed_pair, w_lift, preferred_element_type=jnp.float32
        )
        hidden = (jax.nn.silu(gate_proj) * lift_proj).astype(jnp.bfloat16)
        return (
            summed + jnp.einsum("ijf,fc->ijc", hidden, w_drop, preferred_element_type=jnp.float32)
        ).astype(jnp.bfloat16)

    pair_out = lax.map(
        pair_block,
        (
            left_rows.reshape(-1, step_rows, left_rows.shape[1]),
            pair_state.reshape(-1, step_rows, col_tokens, pair_width),
        ),
    )
    return (atom_out, token_single, pair_out.reshape(row_tokens, col_tokens, pair_width))


def solution(mesh):
    in_specs = (
        P(("row", "col"), None),
        P(("row", "col")),
        P(),
        P(),
        P(),
        P(),
        P(),
        P(),
        P(),
        P(),
        P("row", "col", None),
        P(),
        P(),
        P(),
        P(),
        P(),
        P(),
        P(),
    )
    out_specs = (P(("row", "col"), None), P(("row", "col"), None), P("row", "col", None))
    return jax.shard_map(
        per_device, mesh=mesh, in_specs=in_specs, out_specs=out_specs, check_vma=False
    )
```

profile of v0, /device:TPU:1, one launch (start us, length us, event | category | flops | bytes accessed | tf_op | source)
XLA Modules:
  0.0 1071.9 jit_solution(7566077309387999252)
XLA Ops:
  9.0 1.0 convolution_convert_fusion.3
  10.0 8.7 collective-permute-start.1
  18.8 1.9 collective-permute-start
  22.1 1.0 reduce-window.9
  24.9 1.0 convolution_convert_fusion.4
  25.9 142.4 %while.37 = (s32[]{:T(128)}, u32[2048]{0:T(1024)S(1)}, u32[2048]{0:T(1024)S(1)}, s32[2048]{0:T(1024)S(1)}, s32[2048]{0:T(1024)S(1)}, /*index=5*/s32[]{:T(128)}, s32[]{:T(128)}, s32[]{}) while((s32[]{:T(128)}, u32[2048]{0:T(1024)S(1)}, u32[2048]{0:T(1024)S(1)}, s32[2048]{0:T(1024)S(1)}, s32[2048]{0:T(1024)S(1)}, ...), condition=%wide.region_7.8_spmd.clone, body=%wide.region_6.7_spmd.clone.sunk | while | flops 38916 | bytes 135277 | solution.py:129
  25.9 11.8 %gather_fusion = s32[2048]{0:T(1024)S(1)} fusion(s32[2048]{0:T(1024)S(1)} %get-tuple-element.368, u32[2048]{0:T(1024)S(1)} %broadcast_clamp_fusion.3), kind=kCustom, calls=%fused_computation.clone.clone.1 | custom fusion | bytes 24576 | tf_op jit(solution)/shard_map/jit(searchsorted)/jit(_searchsorted_scan_impl)/vmap(jit(_searchsorted_scan_impl))/while/body/eval_jaxpr/gather | solution.py:129
  37.8 11.8 %gather_fusion = s32[2048]{0:T(1024)S(1)} fusion(s32[2048]{0:T(1024)S(1)} %get-tuple-element.368, u32[2048]{0:T(1024)S(1)} %broadcast_clamp_fusion.3), kind=kCustom, calls=%fused_computation.clone.clone.1 | custom fusion | bytes 24576 | tf_op jit(solution)/shard_map/jit(searchsorted)/jit(_searchsorted_scan_impl)/vmap(jit(_searchsorted_scan_impl))/while/body/eval_jaxpr/gather | solution.py:129
  49.6 11.8 %gather_fusion = s32[2048]{0:T(1024)S(1)} fusion(s32[2048]{0:T(1024)S(1)} %get-tuple-element.368, u32[2048]{0:T(1024)S(1)} %broadcast_clamp_fusion.3), kind=kCustom, calls=%fused_computation.clone.clone.1 | custom fusion | bytes 24576 | tf_op jit(solution)/shard_map/jit(searchsorted)/jit(_searchsorted_scan_impl)/vmap(jit(_searchsorted_scan_impl))/while/body/eval_jaxpr/gather | solution.py:129
  61.5 11.8 %gather_fusion = s32[2048]{0:T(1024)S(1)} fusion(s32[2048]{0:T(1024)S(1)} %get-tuple-element.368, u32[2048]{0:T(1024)S(1)} %broadcast_clamp_fusion.3), kind=kCustom, calls=%fused_computation.clone.clone.1 | custom fusion | bytes 24576 | tf_op jit(solution)/shard_map/jit(searchsorted)/jit(_searchsorted_scan_impl)/vmap(jit(_searchsorted_scan_impl))/while/body/eval_jaxpr/gather | solution.py:129
  73.4 11.8 %gather_fusion = s32[2048]{0:T(1024)S(1)} fusion(s32[2048]{0:T(1024)S(1)} %get-tuple-element.368, u32[2048]{0:T(1024)S(1)} %broadcast_clamp_fusion.3), kind=kCustom, calls=%fused_computation.clone.clone.1 | custom fusion | bytes 24576 | tf_op jit(solution)/shard_map/jit(searchsorted)/jit(_searchsorted_scan_impl)/vmap(jit(_searchsorted_scan_impl))/while/body/eval_jaxpr/gather | solution.py:129
  85.2 11.8 %gather_fusion = s32[2048]{0:T(1024)S(1)} fusion(s32[2048]{0:T(1024)S(1)} %get-tuple-element.368, u32[2048]{0:T(1024)S(1)} %broadcast_clamp_fusion.3), kind=kCustom, calls=%fused_computation.clone.clone.1 | custom fusion | bytes 24576 | tf_op jit(solution)/shard_map/jit(searchsorted)/jit(_searchsorted_scan_impl)/vmap(jit(_searchsorted_scan_impl))/while/body/eval_jaxpr/gather | solution.py:129
  97.1 11.8 %gather_fusion = s32[2048]{0:T(1024)S(1)} fusion(s32[2048]{0:T(1024)S(1)} %get-tuple-element.368, u32[2048]{0:T(1024)S(1)} %broadcast_clamp_fusion.3), kind=kCustom, calls=%fused_computation.clone.clone.1 | custom fusion | bytes 24576 | tf_op jit(solution)/shard_map/jit(searchsorted)/jit(_searchsorted_scan_impl)/vmap(jit(_searchsorted_scan_impl))/while/body/eval_jaxpr/gather | solution.py:129
  109.0 11.8 %gather_fusion = s32[2048]{0:T(1024)S(1)} fusion(s32[2048]{0:T(1024)S(1)} %get-tuple-element.368, u32[2048]{0:T(1024)S(1)} %broadcast_clamp_fusion.3), kind=kCustom, calls=%fused_computation.clone.clone.1 | custom fusion | bytes 24576 | tf_op jit(solution)/shard_map/jit(searchsorted)/jit(_searchsorted_scan_impl)/vmap(jit(_searchsorted_scan_impl))/while/body/eval_jaxpr/gather | solution.py:129
  120.8 11.8 %gather_fusion = s32[2048]{0:T(1024)S(1)} fusion(s32[2048]{0:T(1024)S(1)} %get-tuple-element.368, u32[2048]{0:T(1024)S(1)} %broadcast_clamp_fusion.3), kind=kCustom, calls=%fused_computation.clone.clone.1 | custom fusion | bytes 24576 | tf_op jit(solution)/shard_map/jit(searchsorted)/jit(_searchsorted_scan_impl)/vmap(jit(_searchsorted_scan_impl))/while/body/eval_jaxpr/gather | solution.py:129
  132.7 11.8 %gather_fusion = s32[2048]{0:T(1024)S(1)} fusion(s32[2048]{0:T(1024)S(1)} %get-tuple-element.368, u32[2048]{0:T(1024)S(1)} %broadcast_clamp_fusion.3), kind=kCustom, calls=%fused_computation.clone.clone.1 | custom fusion | bytes 24576 | tf_op jit(solution)/shard_map/jit(searchsorted)/jit(_searchsorted_scan_impl)/vmap(jit(_searchsorted_scan_impl))/while/body/eval_jaxpr/gather | solution.py:129
  144.6 11.8 %gather_fusion = s32[2048]{0:T(1024)S(1)} fusion(s32[2048]{0:T(1024)S(1)} %get-tuple-element.368, u32[2048]{0:T(1024)S(1)} %broadcast_clamp_fusion.3), kind=kCustom, calls=%fused_computation.clone.clone.1 | custom fusion | bytes 24576 | tf_op jit(solution)/shard_map/jit(searchsorted)/jit(_searchsorted_scan_impl)/vmap(jit(_searchsorted_scan_impl))/while/body/eval_jaxpr/gather | solution.py:129
  156.4 11.8 %gather_fusion = s32[2048]{0:T(1024)S(1)} fusion(s32[2048]{0:T(1024)S(1)} %get-tuple-element.368, u32[2048]{0:T(1024)S(1)} %broadcast_clamp_fusion.3), kind=kCustom, calls=%fused_computation.clone.clone.1 | custom fusion | bytes 24576 | tf_op jit(solution)/shard_map/jit(searchsorted)/jit(_searchsorted_scan_impl)/vmap(jit(_searchsorted_scan_impl))/while/body/eval_jaxpr/gather | solution.py:129
  174.9 2.4 collective-permute-start.2
  177.4 2.4 collective-permute-done.2
  180.7 831.9 %all-gather.2.cloned.1.call-done = bf16[4096,384]{1,0:T(8,128)(2,1)} async-done(((bf16[8,384]{1,0:T(8,128)(2,1)}), bf16[4096,384]{1,0:T(8,128)(2,1)}) %all-gather.2.cloned.1.call-update) | async-done | bytes 3145744 | tf_op jit(solution)/shard_map/all_gather | solution.py:131
  1012.6 9.5 gather_fusion.1
  1023.0 1.4 fusion.19
  1027.6 37.5 %while.35 = (s32[]{:T(128)}, bf16[8,8,128,128]{3,2,1,0:T(8,128)(2,1)}, bf16[8,8,128,128]{3,2,1,0:T(8,128)(2,1)}, bf16[8,8,32]{2,1,0:T(8,128)(2,1)S(1)}, bf16[128...) while((s32[]{:T(128)}, ...), condition=%wide.region_13.14_spmd, body=%wide.region_10.13_spmd.sunk | while | flops 415761408 | bytes 12229241 | solution.py:172
  1027.6 1.0 constant_dynamic-slice_fusion.5
  1032.3 1.0 constant_dynamic-slice_fusion.5
  1037.0 1.0 constant_dynamic-slice_fusion.5
  1041.7 1.0 constant_dynamic-slice_fusion.5
  1046.4 1.0 constant_dynamic-slice_fusion.5
  1051.1 1.0 constant_dynamic-slice_fusion.5
  1055.7 1.0 constant_dynamic-slice_fusion.5
  1060.4 1.0 constant_dynamic-slice_fusion.5
  (197 shorter events, 43.0 us)
Async XLA Ops:
  7.2 1019.2 %copy-start = (bf16[32,32,128]{2,1,0:T(8,128)(2,1)S(1)}, bf16[32,32,128]{2,1,0:T(8,128)(2,1)}, u32[]{:S(2)}) copy-start(bf16[32,32,128]{2,1,0:T(8,128)(2,1)} %param.35) | copy-start | bytes 786436
  7.2 1005.4 %all-gather.2.cloned.1.call-start = ((), (), s32[]{:S(2)}) async-start(), calls=%async_computation | async-start | bytes 3151872 | tf_op jit(solution)/shard_map/all_gather | solution.py:131
  10.0 163.3 %collective-permute-start.1 = (bf16[64,256]{1,0:T(8,128)(2,1)S(1)}, bf16[64,256]{1,0:T(8,128)(2,1)S(1)}, u32[]{:S(2)}, u32[]{:S(2)}) collective-permute-start(bf16[64,256]{1,0:T(8,128)(2,1)S(1)} %convolution_convert_fusion.3), channel_id=1, source_target_pairs={{1,0},{2,1},{3,2},{4,3},{5,4},{6,5},{7,6},{8,7},{9,8},{10,9},{11,1... | collective-permute-start | bytes 98312 | tf_op jit(solution)/shard_map/ppermute | solution.py:25
  18.8 154.5 %collective-permute-start = (bf16[64,256]{1,0:T(8,128)(2,1)S(1)}, bf16[64,256]{1,0:T(8,128)(2,1)S(1)}, u32[]{:S(2)}, u32[]{:S(2)}) collective-permute-start(bf16[64,256]{1,0:T(8,128)(2,1)S(1)} %convolution_convert_fusion.3), channel_id=1, source_target_pairs={{0,1},{1,2},{2,3},{3,4},{4,5},{5,6},{6,7},{7,8},{8,9},{9,10},{10,1... | collective-permute-start | bytes 98312 | tf_op jit(solution)/shard_map/ppermute | solution.py:22
  168.3 6.2 copy-start.3
  168.3 6.2 copy-start.5
  168.3 6.3 copy-start.4
  174.9 4.9 collective-permute-start.2
  1022.1 0.9 copy-start.10
  1022.1 2.9 copy-start.6
  1023.0 2.6 copy-start.7
  1026.2 1.4 copy-start.1
  1026.2 1.4 copy-start.2
  1026.2 1.4 copy-start.8
  1026.2 1.4 copy-start.9
Sparse Core Ops, SparseCore 0:
  180.8 831.7 all-gather.1
where the time goes:
time: 1080 us; the launch traced here: 1070 us
  waiting for transfers between devices  834 us (77%)
  local copies, waits for them, and re-layouts  168 us (16%)
  matrix products  24.3 us (2%)
  between operations  17.7 us (2%)
  other arithmetic  13.9 us (1%)
  starting transfers between devices  13.1 us (1%)
    all_gather x1, waiting for transfers between devices, per_device(): gathered = lax.all_gather(slot_single, ('row', 'col'), axis=0, tiled=True)  832 us
    gather x12, local copies, waits for them, and re-layouts, per_device(): owner_first = jnp.searchsorted(token_starts, owner * atom_rows, side='left')  141 us
  transfers between devices with their start and end apart: 4, of which 2 were waited for; matrix products, arithmetic and copies ran while one was open for 14% of the time, Pallas kernels for 0%

commit v1 on v0

v1 whole, which is shorter than its diff:
```python
import math

import jax
import jax.numpy as jnp
from jax import lax
from jax.sharding import PartitionSpec as P

HEADS = 4
QB = 32
KW = 128
FEWEST = 8
MOST = 24
EPSILON = 1e-05
BOTH = ("row", "col")


def shifted(block, distance):
    count = lax.axis_size(BOTH)
    route = [(i - distance, i) for i in range(count) if 0 <= i - distance < count]
    return lax.ppermute(block, BOTH, route)


def layer_norm(values, gain):
    mean_value = jnp.mean(values, axis=-1, keepdims=True)
    centred = values - mean_value
    variance = jnp.mean(centred * centred, axis=-1, keepdims=True)
    return centred * lax.rsqrt(variance + EPSILON) * gain


def project(source, weight):
    return jnp.dot(source, weight, preferred_element_type=jnp.float32).astype(jnp.bfloat16)


def atom_part(ext, feats_q, starts, first_atom, total_atoms, spans, atom_gain, w_query, w_key,
              w_value, w_out, w_pool, w_back):
    width = ext.shape[1]
    head = width // HEADS
    normed = layer_norm(ext.astype(jnp.float32), atom_gain).astype(jnp.bfloat16)
    keys = project(normed, w_key)
    values = project(normed, w_value)
    queries = project(normed[64:192], w_query)
    key_atom = first_atom - 96 + lax.broadcasted_iota(jnp.int32, (128, 256), 1)
    mask = (key_atom >= starts) & (key_atom < starts + KW) & (key_atom >= 0) & (key_atom < total_atoms)
    query_atom = first_atom - 32 + lax.broadcasted_iota(jnp.int32, (128, 1), 0)
    real = (query_atom >= 0) & (query_atom < total_atoms)
    pieces = []
    for h in range(HEADS):
        cut = slice(h * head, (h + 1) * head)
        scores = lax.dot_general(queries[:, cut], keys[:, cut], (((1,), (1,)), ((), ())),
                                 preferred_element_type=jnp.float32) * head ** (-0.5)
        raised = jnp.where(mask, jnp.exp(scores), 0.0)
        total = jnp.where(real, jnp.sum(raised, axis=-1, keepdims=True), 1.0)
        weights = (raised / total).astype(jnp.bfloat16)
        pieces.append(jnp.dot(weights, values[:, cut], preferred_element_type=jnp.float32))
    attended = jnp.concatenate(pieces, axis=1).astype(jnp.bfloat16)
    updated = (feats_q.astype(jnp.float32)
               + jnp.dot(attended, w_out, preferred_element_type=jnp.float32)).astype(jnp.bfloat16)
    feature = jax.nn.relu(jnp.dot(updated, w_pool, preferred_element_type=jnp.float32)).astype(jnp.bfloat16)
    low, high = spans
    atoms = first_atom - 32 + lax.broadcasted_iota(jnp.int32, (low.shape[0], 128), 1)
    member = ((atoms >= low) & (atoms < high)).astype(jnp.bfloat16)
    pooled = jnp.dot(member, feature, preferred_element_type=jnp.float32)
    counts = jnp.maximum(high - low, 1).astype(jnp.float32)
    single = (pooled / counts).astype(jnp.bfloat16)
    back = project(single, w_back)
    lifted = lax.dot_general(member[:, 32:96], back, (((0,), (0,)), ((), ())),
                             preferred_element_type=jnp.float32)
    atom_out = (updated[32:96].astype(jnp.float32) + lifted).astype(jnp.bfloat16)
    return atom_out, single


def per_device(
    atom_feats,
    key_starts,
    atom_counts,
    atom_gain,
    w_query,
    w_key,
    w_value,
    w_out,
    w_pool,
    w_back,
    pair_state,
    w_left,
    w_right,
    w_outer,
    pair_gain,
    w_gate,
    w_lift,
    w_drop,
):
    atom_rows, atom_width = atom_feats.shape
    devices = lax.axis_size(BOTH)
    rows, cols = lax.axis_size("row"), lax.axis_size("col")
    row, col = lax.axis_index("row"), lax.axis_index("col")
    position = row * cols + col
    total_atoms = atom_rows * devices
    total_tokens = atom_counts.shape[0]
    first_atom = position * atom_rows
    blocks = atom_rows // QB
    offsets = key_starts - (QB * (position * blocks + jnp.arange(blocks, dtype=jnp.int32)) - KW // 2)
    offset_rows = jnp.zeros((8, atom_width), jnp.bfloat16).at[:blocks].set(
        jnp.broadcast_to(offsets[:, None], (blocks, atom_width)).astype(jnp.bfloat16))
    packed = jnp.concatenate([atom_feats, offset_rows], axis=0)
    prev1, next1 = shifted(packed, 1), shifted(packed, -1)
    prev2, next2 = shifted(atom_feats[32:], 2), shifted(atom_feats[:32], -2)

    token_ends = jnp.cumsum(atom_counts, dtype=jnp.int32)
    token_starts = token_ends - atom_counts
    edges = atom_rows * jnp.arange(devices + 1, dtype=jnp.int32)
    bases = jnp.sum((token_starts[None, :] < edges[:, None]).astype(jnp.int32), axis=1)
    base = lax.dynamic_index_in_dim(bases, position, 0, keepdims=False)
    pad = jnp.full((16,), total_atoms, jnp.int32)
    padded_starts = jnp.concatenate([jnp.zeros((1,), jnp.int32) - MOST, token_starts, pad])
    padded_ends = jnp.concatenate([jnp.zeros((1,), jnp.int32), token_ends, pad])
    low = lax.dynamic_slice_in_dim(padded_starts, base, 16, 0)[:, None]
    high = lax.dynamic_slice_in_dim(padded_ends, base, 16, 0)[:, None]

    ext = jnp.concatenate([prev2, prev1[:64], atom_feats, next1[:64], next2], axis=0)
    feats_q = jnp.concatenate([prev1[32:64], atom_feats, next1[:32]], axis=0)
    off4 = jnp.concatenate([prev1[65:66, :1], offset_rows[0:2, :1], next1[64:65, :1]], axis=0)
    starts4 = off4.astype(jnp.int32) + first_atom - QB - KW // 2 + QB * jnp.arange(4, dtype=jnp.int32)[:, None]
    starts = jnp.repeat(starts4, QB, axis=0)
    atom_out, single = atom_part(ext, feats_q, starts, first_atom, total_atoms, (low, high), atom_gain,
                                 w_query, w_key, w_value, w_out, w_pool, w_back)
    slots = atom_rows // FEWEST
    slot_single = single[1:1 + slots]

    slot_index = jnp.arange(slots, dtype=jnp.int32)[None, :]
    token_id = jnp.where(slot_index < (bases[1:] - bases[:-1])[:, None], bases[:-1, None] + slot_index, -1)
    row_slots = cols * slots
    row_single = lax.all_gather(slot_single, "col", axis=0, tiled=True)
    row_ids = lax.dynamic_slice_in_dim(token_id.reshape(rows, row_slots), row, 1, 0)
    lr = project(row_single, jnp.concatenate([w_left, w_right], axis=1))
    gathered = lax.all_gather(lr, "row", axis=0, tiled=True)
    opm = w_left.shape[1]
    row_tokens, col_tokens, pair_width = pair_state.shape

    all_ids = token_id.reshape(1, -1)
    want_left = row * row_tokens + jnp.arange(row_tokens, dtype=jnp.int32)[:, None]
    want_right = col * col_tokens + jnp.arange(col_tokens, dtype=jnp.int32)[:, None]
    left_rows = project((all_ids == want_left).astype(jnp.bfloat16), gathered[:, :opm])
    right_cols = project((all_ids == want_right).astype(jnp.bfloat16), gathered[:, opm:])

    own = total_tokens // devices
    place = jnp.arange(rows * own, dtype=jnp.int32)
    want_own = ((place // own) * cols + col) * own + place % own
    spread = project((row_ids == want_own[:, None]).astype(jnp.bfloat16), row_single)
    token_single = lax.psum_scatter(spread, "row", scatter_dimension=0, tiled=True)

    outer_table = jnp.einsum(
        "jb,abc->jac", right_cols, w_outer, preferred_element_type=jnp.float32
    ).astype(jnp.bfloat16)
    step_rows = math.gcd(row_tokens, 8)

    def pair_block(pieces):
        left_block, pair_piece = pieces
        outer_term = jnp.einsum(
            "ia,jac->ijc", left_block, outer_table, preferred_element_type=jnp.float32
        )
        summed = pair_piece.astype(jnp.float32) + outer_term
        normed_pair = layer_norm(summed, pair_gain).astype(jnp.bfloat16)
        gate_proj = jnp.einsum(
            "ijc,cf->ijf", normed_pair, w_gate, preferred_element_type=jnp.float32
        )
        lift_proj = jnp.einsum(
            "ijc,cf->ijf", normed_pair, w_lift, preferred_element_type=jnp.float32
        )
        hidden = (jax.nn.silu(gate_proj) * lift_proj).astype(jnp.bfloat16)
        return (
            summed + jnp.einsum("ijf,fc->ijc", hidden, w_drop, preferred_element_type=jnp.float32)
        ).astype(jnp.bfloat16)

    pair_out = lax.map(
        pair_block,
        (
            left_rows.reshape(-1, step_rows, left_rows.shape[1]),
            pair_state.reshape(-1, step_rows, col_tokens, pair_width),
        ),
    )
    return (atom_out, token_single, pair_out.reshape(row_tokens, col_tokens, pair_width))


def solution(mesh):
    whole = P(BOTH, None)
    in_specs = (whole, P(BOTH)) + (P(),) * 8 + (P("row", "col", None),) + (P(),) * 7
    out_specs = (whole, whole, P("row", "col", None))
    return jax.shard_map(
        per_device, mesh=mesh, in_specs=in_specs, out_specs=out_specs, check_vma=False
    )
```

time: 1080 us -> 334 us (0.31)
  the two profiles are of different devices: /device:TPU:1 before, /device:TPU:2 now
where the time goes in v1:
time: 334 us; the launch traced here: 333 us
  waiting for transfers between devices  147 us (44%)
  blocking collectives  93.9 us (28%)
  matrix products  26.1 us (8%)
  local copies, waits for them, and re-layouts  21.3 us (6%)
  between operations  17.1 us (5%)
  starting transfers between devices  14.1 us (4%)
  other arithmetic  12.9 us (4%)
    unnamed x2, waiting for transfers between devices  147 us
    all_gather x1, blocking collectives, per_device(): gathered = lax.all_gather(lr, 'row', axis=0, tiled=True)  72.7 us
    all_gather x1, blocking collectives, per_device(): row_single = lax.all_gather(slot_single, 'col', axis=0, tiled=True)  21.2 us
    ppermute x4, starting transfers between devices, shifted(): return lax.ppermute(block, BOTH, route)  14 us
    dynamic_slice x8, local copies, waits for them, and re-layouts, per_device(): lax.map(pair_block, (left_rows.reshape(-1, step_rows, left_rows.shape[1])...  7.78 us
  transfers between devices with their start and end apart: 5, of which 1 were waited for; matrix products, arithmetic and copies ran while one was open for 15% of the time, Pallas kernels for 0%

profile of v1, /device:TPU:2, one launch (start us, length us, event | category | flops | bytes accessed | tf_op | source)
XLA Modules:
  0.0 333.0 jit_solution(10406786678176366872)
XLA Ops:
  8.0 0.8 pad_maximum_fusion
  8.8 1.9 collective-permute-start.1
  10.7 2.4 collective-permute-start
  13.8 7.8 %collective-permute-start.3 = (bf16[32,128]{1,0:T(8,128)(2,1)S(1)}, bf16[32,128]{1,0:T(8,128)(2,1)S(1)}, u32[]{:S(2)}, u32[]{:S(2)}) collective-permute-start(bf16[32,128]{1,0:T(8,128)(2,1)S(1)} %get-tuple-element.133), channel_id=1, source_target_pairs={{2,0},{3,1},{4,2},{5,3},{6,4},{7,5},{8,6},{9,7},{10,8},{11,9},{12,... | collective-permute-start | bytes 24584 | tf_op jit(solution)/shard_map/ppermute | solution.py:20
  21.6 1.9 collective-permute-start.2
  23.6 1.0 reduce-window.9
  24.8 0.8 fusion.93
  30.2 1.3 dynamic-slice.6
  33.2 1.4 fusion.89
  35.8 0.8 fusion.47
  36.6 1.0 convolution_convert_fusion.4
  37.6 1.0 convolution_convert_fusion.3
  41.5 21.2 %all_gather.6 = bf16[128,384]{1,0:T(8,128)(2,1)S(1)} all-gather(bf16[8,384]{1,0:T(8,128)(2,1)S(1)} %slice.169), channel_id=1, replica_groups=mesh['row'=32,'col'=16] {'col'}, dimensions={0}, use_global_device_ids=true | all-gather | bytes 104448 | tf_op jit(solution)/shard_map/all_gather | solution.py:132
  62.7 0.9 convolution_convert_fusion.1
  63.8 72.7 %all_gather.7 = bf16[4096,64]{0,1:T(8,128)(2,1)S(1)} all-gather(bf16[128,64]{0,1:T(8,128)(2,1)S(1)} %convolution_convert_fusion.5), channel_id=1, replica_groups=mesh['row'=32,'col'=16] {'row'}, dimensions={0}, use_global_device_ids=true | all-gather | bytes 540672 | tf_op jit(solution)/shard_map/all_gather | solution.py:135
  136.9 1.4 convolution_convert_fusion
  139.1 37.6 %while.11 = (s32[]{:T(128)}, bf16[8,8,128,128]{3,2,1,0:T(8,128)(2,1)}, bf16[8,8,128,128]{3,2,1,0:T(8,128)(2,1)}, bf16[8,8,32]{2,1,0:T(8,128)(2,1)S(1)}, bf16[128...) while((s32[]{:T(128)}, ...), condition=%wide.region_13.14_spmd, body=%wide.region_10.13_spmd.sunk | while | flops 415761408 | bytes 12229241 | solution.py:174
  139.1 1.0 constant_dynamic-slice_fusion.3
  143.9 1.0 constant_dynamic-slice_fusion.3
  147.8 0.7 copy_dynamic-update-slice_fusion.2
  148.5 1.0 constant_dynamic-slice_fusion.3
  152.5 0.7 copy_dynamic-update-slice_fusion.2
  153.2 1.0 constant_dynamic-slice_fusion.3
  157.2 0.7 copy_dynamic-update-slice_fusion.2
  157.9 1.0 constant_dynamic-slice_fusion.3
  161.9 0.7 copy_dynamic-update-slice_fusion.2
  162.6 1.0 constant_dynamic-slice_fusion.3
  167.3 1.0 constant_dynamic-slice_fusion.3
  172.0 1.0 constant_dynamic-slice_fusion.3
  176.7 0.9 fusion.24
  177.6 147.3 %all-reduce.4.cloned.1.call-done = bf16[128,384]{1,0:T(8,128)(2,1)} async-done(((bf16[128,384]{1,0:T(8,128)(2,1)}), bf16[128,384]{1,0:T(8,128)(2,1)}) %all-reduce.4.cloned.1.call-update) | async-done | bytes 98320
  324.9 1.3 constant_dynamic-slice_fusion.1
  (167 shorter events, 37.1 us)
Async XLA Ops:
  7.2 129.8 %copy-start = (bf16[32,32,128]{2,1,0:T(8,128)(2,1)S(1)}, bf16[32,32,128]{2,1,0:T(8,128)(2,1)}, u32[]{:S(2)}) copy-start(bf16[32,32,128]{2,1,0:T(8,128)(2,1)} %param.35) | copy-start | bytes 786436
  7.2 32.6 %copy-start.5 = (bf16[128,128]{1,0:T(8,128)(2,1)S(1)}, bf16[128,128]{1,0:T(8,128)(2,1)}, u32[]{:S(2)}) copy-start(bf16[128,128]{1,0:T(8,128)(2,1)} %param.28) | copy-start | bytes 98308
  7.2 317.7 %all-reduce.4.cloned.1.call-start = ((), (), s32[]{:S(2)}) async-start(), calls=%async_computation | async-start | bytes 196608
  8.8 23.4 %collective-permute-start.1 = (bf16[72,128]{1,0:T(8,128)(2,1)S(1)}, bf16[72,128]{1,0:T(8,128)(2,1)S(1)}, u32[]{:S(2)}, u32[]{:S(2)}) collective-permute-start(bf16[72,128]{1,0:T(8,128)(2,1)S(1)} %pad_maximum_fusion), channel_id=1, source_target_pairs={{1,0},{2,1},{3,2},{4,3},{5,4},{6,5},{7,6},{8,7},{9,8},{10,9},{11,1... | collective-permute-start | bytes 55304 | tf_op jit(solution)/shard_map/ppermute | solution.py:20
  10.7 22.0 %collective-permute-start = (bf16[72,128]{1,0:T(8,128)(2,1)S(1)}, bf16[72,128]{1,0:T(8,128)(2,1)S(1)}, u32[]{:S(2)}, u32[]{:S(2)}) collective-permute-start(bf16[72,128]{1,0:T(8,128)(2,1)S(1)} %pad_maximum_fusion), channel_id=1, source_target_pairs={{0,1},{1,2},{2,3},{3,4},{4,5},{5,6},{6,7},{7,8},{8,9},{9,10},{10,1... | collective-permute-start | bytes 55304 | tf_op jit(solution)/shard_map/ppermute | solution.py:20
  13.8 21.6 %collective-permute-start.3 = (bf16[32,128]{1,0:T(8,128)(2,1)S(1)}, bf16[32,128]{1,0:T(8,128)(2,1)S(1)}, u32[]{:S(2)}, u32[]{:S(2)}) collective-permute-start(bf16[32,128]{1,0:T(8,128)(2,1)S(1)} %get-tuple-element.133), channel_id=1, source_target_pairs={{2,0},{3,1},{4,2},{5,3},{6,4},{7,5},{8,6},{9,7},{10,8},{11,9},{12,... | collective-permute-start | bytes 24584 | tf_op jit(solution)/shard_map/ppermute | solution.py:20
  21.6 10.5 %collective-permute-start.2 = (bf16[32,128]{1,0:T(8,128)(2,1)S(1)}, bf16[32,128]{1,0:T(8,128)(2,1)S(1)}, u32[]{:S(2)}, u32[]{:S(2)}) collective-permute-start(bf16[32,128]{1,0:T(8,128)(2,1)S(1)} %get-tuple-element.134), channel_id=1, source_target_pairs={{0,2},{1,3},{2,4},{3,5},{4,6},{5,7},{6,8},{7,9},{8,10},{9,11},{10,... | collective-permute-start | bytes 24584 | tf_op jit(solution)/shard_map/ppermute | solution.py:20
  32.1 8.9 %copy-start.3 = (bf16[64,128]{1,0:T(8,128)(2,1)S(1)}, bf16[64,128]{1,0:T(8,128)(2,1)}, u32[]{:S(2)}) copy-start(bf16[64,128]{1,0:T(8,128)(2,1)} %param.22) | copy-start | bytes 49156
  32.1 8.9 %copy-start.11 = (bf16[128,128]{1,0:T(8,128)(2,1)S(1)}, bf16[128,128]{1,0:T(8,128)(2,1)}, u32[]{:S(2)}) copy-start(bf16[128,128]{1,0:T(8,128)(2,1)} %param.29) | copy-start | bytes 98308
  35.6 5.6 %copy-start.10 = (bf16[128,384]{1,0:T(8,128)(2,1)S(1)}, bf16[128,384]{1,0:T(8,128)(2,1)}, u32[]{:S(2)}) copy-start(bf16[128,384]{1,0:T(8,128)(2,1)} %param.30) | copy-start | bytes 294916
  38.9 24.7 %copy-start.6 = (bf16[384,32]{0,1:T(8,128)(2,1)S(1)}, bf16[384,32]{0,1:T(8,128)(2,1)}, u32[]{:S(2)}) copy-start(bf16[384,32]{0,1:T(8,128)(2,1)} %param.34) | copy-start | bytes 73732
  38.9 24.7 %copy-start.7 = (bf16[384,32]{0,1:T(8,128)(2,1)S(1)}, bf16[384,32]{0,1:T(8,128)(2,1)}, u32[]{:S(2)}) copy-start(bf16[384,32]{0,1:T(8,128)(2,1)} %param.33) | copy-start | bytes 73732
  136.4 2.6 copy-start.1
  136.4 2.6 copy-start.2
  136.4 2.6 copy-start.8
  136.4 2.7 copy-start.9
  139.1 37.6 %copy-start.4 = (bf16[384,128]{1,0:T(8,128)(2,1)S(1)}, bf16[384,128]{1,0:T(8,128)(2,1)}, u32[]{:S(2)}) copy-start(bf16[384,128]{1,0:T(8,128)(2,1)} %param.31) | copy-start | bytes 294916
Sparse Core Ops, SparseCore 0:
  63.7 261.1 all-reduce.3

commit v2 on v1

--- a/solution.py
+++ b/solution.py
@@ -1,9 +1,14 @@
-import math
+import functools
 
 import jax
 import jax.numpy as jnp
 from jax import lax
+from jax.experimental import pallas as pl
+from jax.experimental.pallas import tpu as pltpu
 from jax.sharding import PartitionSpec as P
+
+MESH = pl.DeviceIdType.MESH
+VMEM = pl.BlockSpec(memory_space=pltpu.VMEM)
 
 HEADS = 4
 QB = 32
@@ -69,6 +74,155 @@
     return atom_out, single
 
 
+def spread_kernel(rows, cols, own, ids_col, ids_row, lr_ref, single_ref, lr_out, ts_out,
+                  lbuf, gbuf, lall, gall, lsend, lrecv, tsend, trecv,
+                  s1, r1, s2, r2, s3, r3, s4, r4):
+    row, col = lax.axis_index("row"), lax.axis_index("col")
+    slots = single_ref.shape[0]
+    barrier = pltpu.get_barrier_semaphore()
+
+    def hail_rows(k, _):
+        pl.semaphore_signal(barrier, inc=1, device_id=(lax.rem(row + k, rows), col), device_id_type=MESH)
+        return 0
+
+    def hail_cols(k, _):
+        pl.semaphore_signal(barrier, inc=1, device_id=(row, lax.rem(col + k, cols)), device_id_type=MESH)
+        return 0
+
+    lax.fori_loop(1, rows, hail_rows, 0)
+    lax.fori_loop(1, cols, hail_cols, 0)
+    pl.semaphore_wait(barrier, rows + cols - 2)
+
+    def push_row(src, buf, send, recv, k):
+        return pltpu.make_async_remote_copy(
+            src_ref=src, dst_ref=buf.at[row], send_sem=send.at[k], recv_sem=recv.at[row],
+            device_id=(lax.rem(row + k, rows), col), device_id_type=MESH)
+
+    def from_row(src, buf, send, recv, k):
+        peer = lax.rem(row + k, rows)
+        return pltpu.make_async_remote_copy(
+            src_ref=src, dst_ref=buf.at[peer], send_sem=send.at[k], recv_sem=recv.at[peer],
+            device_id=(peer, col), device_id_type=MESH)
+
+    def push_col(src, buf, send, recv, k):
+        peer = lax.rem(col + k, cols)
+        return pltpu.make_async_remote_copy(
+            src_ref=src.at[peer], dst_ref=buf.at[col], send_sem=send.at[k], recv_sem=recv.at[col],
+            device_id=(row, peer), device_id_type=MESH)
+
+    def from_col(src, buf, send, recv, k):
+        peer = lax.rem(col + k, cols)
+        return pltpu.make_async_remote_copy(
+            src_ref=src.at[peer], dst_ref=buf.at[peer], send_sem=send.at[k], recv_sem=recv.at[peer],
+            device_id=(row, peer), device_id_type=MESH)
+
+    def each(count, act):
+        def body(k, _):
+            act(k)
+            return 0
+        lax.fori_loop(1, count, body, 0)
+
+    each(rows, lambda k: push_row(lr_ref, lbuf, s1, r1, k).start())
+    each(rows, lambda k: push_row(single_ref, gbuf, s2, r2, k).start())
+    lbuf[row] = lr_ref[...]
+    gbuf[row] = single_ref[...]
+    tokens = cols * 128
+    hot = (ids_col[...] == lax.broadcasted_iota(jnp.int32, (rows * slots, tokens), 1)).astype(jnp.bfloat16)
+    hot_left = (ids_col[...] == row * (own * cols)
+                + lax.broadcasted_iota(jnp.int32, (rows * slots, 128), 1)).astype(jnp.bfloat16)
+    each(rows, lambda k: from_row(lr_ref, lbuf, s1, r1, k).wait_recv())
+    for r in range(rows):
+        lall[r * slots:(r + 1) * slots, :] = lbuf[r].astype(jnp.float32)
+    table = lall[...].T.astype(jnp.bfloat16)
+    right = jnp.dot(table[32:64], hot, preferred_element_type=jnp.float32).astype(jnp.bfloat16)
+    left = jnp.dot(table[:32], hot_left, preferred_element_type=jnp.float32).astype(jnp.bfloat16)
+    for c in range(cols):
+        lsend[c, :32] = right[:, c * 128:(c + 1) * 128]
+        lsend[c, 32:] = left
+    each(cols, lambda k: push_col(lsend, lrecv, s3, r3, k).start())
+    lrecv[col] = lsend[col]
+
+    line = lax.broadcasted_iota(jnp.int32, (cols * 8, rows * slots), 0)
+    want = jnp.where(line % 8 < own, row * (own * cols) + (line // 8) * own + line % 8, -2)
+    hot_own = (ids_row[...] == want).astype(jnp.bfloat16)
+    each(rows, lambda k: from_row(single_ref, gbuf, s2, r2, k).wait_recv())
+    for r in range(rows):
+        gall[r * slots:(r + 1) * slots, :] = gbuf[r].astype(jnp.float32)
+    parts = jnp.dot(hot_own, gall[...].astype(jnp.bfloat16), preferred_element_type=jnp.float32)
+    for c in range(cols):
+        tsend[c] = parts[c * 8:(c + 1) * 8].astype(jnp.bfloat16)
+    each(cols, lambda k: push_col(tsend, trecv, s4, r4, k).start())
+    trecv[col] = tsend[col]
+
+    each(cols, lambda k: from_col(lsend, lrecv, s3, r3, k).wait_recv())
+    total = lrecv[0].astype(jnp.float32)
+    for c in range(1, cols):
+        total = total + lrecv[c].astype(jnp.float32)
+    lr_out[...] = total.astype(jnp.bfloat16)
+    each(cols, lambda k: from_col(tsend, trecv, s4, r4, k).wait_recv())
+    total = trecv[0].astype(jnp.float32)
+    for c in range(1, cols):
+        total = total + trecv[c].astype(jnp.float32)
+    ts_out[...] = total.astype(jnp.bfloat16)
+
+    each(rows, lambda k: push_row(lr_ref, lbuf, s1, r1, k).wait_send())
+    each(rows, lambda k: push_row(single_ref, gbuf, s2, r2, k).wait_send())
+    each(cols, lambda k: push_col(lsend, lrecv, s3, r3, k).wait_send())
+    each(cols, lambda k: push_col(tsend, trecv, s4, r4, k).wait_send())
+
+
+def spread(ids_col, ids_row, lr, single, rows, cols, own):
+    slots, width = single.shape
+    kept = jnp.bfloat16
+    return pl.pallas_call(
+        functools.partial(spread_kernel, rows, cols, own),
+        out_shape=(jax.ShapeDtypeStruct((64, 128), kept), jax.ShapeDtypeStruct((8, width), kept)),
+        in_specs=[VMEM] * 4,
+        out_specs=(VMEM, VMEM),
+        scratch_shapes=[
+            pltpu.VMEM((rows, slots, 128), kept),
+            pltpu.VMEM((rows, slots, width), kept),
+            pltpu.VMEM((rows * slots, 128), jnp.float32),
+            pltpu.VMEM((rows * slots, width), jnp.float32),
+            pltpu.VMEM((cols, 64, 128), kept),
+            pltpu.VMEM((cols, 64, 128), kept),
+            pltpu.VMEM((cols, 8, width), kept),
+            pltpu.VMEM((cols, 8, width), kept),
+        ] + [pltpu.SemaphoreType.DMA((rows,))] * 4 + [pltpu.SemaphoreType.DMA((cols,))] * 4,
+        compiler_params=pltpu.CompilerParams(collective_id=0, has_side_effects=True),
+    )(ids_col, ids_row, lr, single)
+
+
+def pair_kernel(pair_ref, table_ref, right_ref, gain_ref, up_ref, drop_ref, out_ref):
+    count, tokens, width = pair_ref.shape
+    right = right_ref[...]
+    outer = jnp.concatenate([
+        jnp.dot(right, table_ref[i], preferred_element_type=jnp.float32) for i in range(count)], axis=0)
+    summed = pair_ref[...].astype(jnp.float32).reshape(count * tokens, width) + outer
+    normed = layer_norm(summed, gain_ref[...]).astype(jnp.bfloat16)
+    raised = jnp.dot(normed, up_ref[...], preferred_element_type=jnp.float32)
+    units = drop_ref.shape[0]
+    half = raised[:, :units]
+    hidden = ((half + half * jnp.tanh(half)) * raised[:, units:]).astype(jnp.bfloat16)
+    total = summed + jnp.dot(hidden, drop_ref[...], preferred_element_type=jnp.float32)
+    out_ref[...] = total.astype(jnp.bfloat16).reshape(count, tokens, width)
+
+
+def pair_update(pair_state, table, right, gain, up, drop):
+    rows, tokens, width = pair_state.shape
+    step = 4
+    whole = lambda a: pl.BlockSpec(a.shape, lambda i: (0,) * a.ndim)
+    tile = pl.BlockSpec((step, tokens, width), lambda i: (i, 0, 0))
+    return pl.pallas_call(
+        pair_kernel,
+        grid=(rows // step,),
+        out_shape=jax.ShapeDtypeStruct(pair_state.shape, pair_state.dtype),
+        in_specs=[tile, pl.BlockSpec((step,) + table.shape[1:], lambda i: (i, 0, 0)), whole(right),
+                  whole(gain), whole(up), whole(drop)],
+        out_specs=tile,
+    )(pair_state, table, right, gain, up, drop)
+
+
 def per_device(
     atom_feats,
     key_starts,
@@ -128,57 +282,19 @@
 
     slot_index = jnp.arange(slots, dtype=jnp.int32)[None, :]
     token_id = jnp.where(slot_index < (bases[1:] - bases[:-1])[:, None], bases[:-1, None] + slot_index, -1)
-    row_slots = cols * slots
-    row_single = lax.all_gather(slot_single, "col", axis=0, tiled=True)
-    row_ids = lax.dynamic_slice_in_dim(token_id.reshape(rows, row_slots), row, 1, 0)
-    lr = project(row_single, jnp.concatenate([w_left, w_right], axis=1))
-    gathered = lax.all_gather(lr, "row", axis=0, tiled=True)
-    opm = w_left.shape[1]
-    row_tokens, col_tokens, pair_width = pair_state.shape
-
-    all_ids = token_id.reshape(1, -1)
-    want_left = row * row_tokens + jnp.arange(row_tokens, dtype=jnp.int32)[:, None]
-    want_right = col * col_tokens + jnp.arange(col_tokens, dtype=jnp.int32)[:, None]
-    left_rows = project((all_ids == want_left).astype(jnp.bfloat16), gathered[:, :opm])
-    right_cols = project((all_ids == want_right).astype(jnp.bfloat16), gathered[:, opm:])
-
+    mine = lax.dynamic_index_in_dim(token_id.reshape(rows, cols, slots), col, 1, keepdims=False).reshape(-1)
+    width = w_left.shape[1]
+    w_both = jnp.concatenate([w_left, w_right, jnp.zeros((w_left.shape[0], 128 - 2 * width), w_left.dtype)], axis=1)
+    lr = project(slot_single, w_both)
     own = total_tokens // devices
-    place = jnp.arange(rows * own, dtype=jnp.int32)
-    want_own = ((place // own) * cols + col) * own + place % own
-    spread = project((row_ids == want_own[:, None]).astype(jnp.bfloat16), row_single)
-    token_single = lax.psum_scatter(spread, "row", scatter_dimension=0, tiled=True)
-
-    outer_table = jnp.einsum(
-        "jb,abc->jac", right_cols, w_outer, preferred_element_type=jnp.float32
-    ).astype(jnp.bfloat16)
-    step_rows = math.gcd(row_tokens, 8)
-
-    def pair_block(pieces):
-        left_block, pair_piece = pieces
-        outer_term = jnp.einsum(
-            "ia,jac->ijc", left_block, outer_table, preferred_element_type=jnp.float32
-        )
-        summed = pair_piece.astype(jnp.float32) + outer_term
-        normed_pair = layer_norm(summed, pair_gain).astype(jnp.bfloat16)
-        gate_proj = jnp.einsum(
-            "ijc,cf->ijf", normed_pair, w_gate, preferred_element_type=jnp.float32
-        )
-        lift_proj = jnp.einsum(
-            "ijc,cf->ijf", normed_pair, w_lift, preferred_element_type=jnp.float32
-        )
-        hidden = (jax.nn.silu(gate_proj) * lift_proj).astype(jnp.bfloat16)
-        return (
-            summed + jnp.einsum("ijf,fc->ijc", hidden, w_drop, preferred_element_type=jnp.float32)
-        ).astype(jnp.bfloat16)
-
-    pair_out = lax.map(
-        pair_block,
-        (
-            left_rows.reshape(-1, step_rows, left_rows.shape[1]),
-            pair_state.reshape(-1, step_rows, col_tokens, pair_width),
-        ),
-    )
-    return (atom_out, token_single, pair_out.reshape(row_tokens, col_tokens, pair_width))
+    turned, token_single = spread(mine[:, None], mine[None, :], lr, slot_single, rows, cols, own)
+    row_tokens = pair_state.shape[0]
+    right = turned[:width].T
+    table = jnp.einsum("ai,abc->ibc", turned[width:2 * width, :row_tokens], w_outer,
+                       preferred_element_type=jnp.float32).astype(jnp.bfloat16)
+    up = jnp.concatenate([w_gate * 0.5, w_lift], axis=1)
+    pair_out = pair_update(pair_state, table, right, pair_gain[None, :], up, w_drop)
+    return atom_out, token_single[:own], pair_out
 
 
 def solution(mesh):

time: 334 us -> 107 us (0.32)
  the two profiles are of different devices: /device:TPU:2 before, /device:TPU:1 now
where the time goes in v2:
time: 107 us; the launch traced here: 106 us
  Pallas kernels  60.8 us (57%)
  starting transfers between devices  15.9 us (15%)
  local copies, waits for them, and re-layouts  11.7 us (11%)
  other arithmetic  9.25 us (9%)
  matrix products  5.88 us (5%)
  between operations  2.93 us (3%)
    pallas_call x1, Pallas kernels, spread(): pl.pallas_call(functools.partial(spread_kernel, rows, cols, own), out_sha...  42.5 us
    pallas_call x1, Pallas kernels, pair_update(): pl.pallas_call(pair_kernel, grid=(rows // step,), out_shape=jax.ShapeDtyp...  18.2 us
    ppermute x4, starting transfers between devices, shifted(): return lax.ppermute(block, BOTH, route)  15.9 us
    unnamed x22, local copies, waits for them, and re-layouts  2.5 us
  transfers between devices with their start and end apart: 4, of which 0 were waited for; matrix products, arithmetic and copies ran while one was open for 13% of the time, Pallas kernels for 0%

profile of v2, /device:TPU:1, one launch (start us, length us, event | category | flops | bytes accessed | tf_op | source)
XLA Modules:
  0.0 106.4 jit_solution(9711530956710218173)
XLA Ops:
  0.7 0.7 subtract_convert_fusion
  1.5 0.8 pad_maximum_fusion.1
  2.3 8.7 %collective-permute-start.1 = (bf16[72,128]{1,0:T(8,128)(2,1)S(1)}, bf16[72,128]{1,0:T(8,128)(2,1)S(1)}, u32[]{:S(2)}, u32[]{:S(2)}) collective-permute-start(bf16[72,128]{1,0:T(8,128)(2,1)S(1)} %pad_maximum_fusion.1), channel_id=1, source_target_pairs={{1,0},{2,1},{3,2},{4,3},{5,4},{6,5},{7,6},{8,7},{9,8},{10,9},{11,1... | collective-permute-start | bytes 55304 | tf_op jit(solution)/shard_map/ppermute | solution.py:25
  11.0 1.9 %collective-permute-start = (bf16[72,128]{1,0:T(8,128)(2,1)S(1)}, bf16[72,128]{1,0:T(8,128)(2,1)S(1)}, u32[]{:S(2)}, u32[]{:S(2)}) collective-permute-start(bf16[72,128]{1,0:T(8,128)(2,1)S(1)} %pad_maximum_fusion.1), channel_id=1, source_target_pairs={{0,1},{1,2},{2,3},{3,4},{4,5},{5,6},{6,7},{7,8},{8,9},{9,10},{10,1... | collective-permute-start | bytes 55304 | tf_op jit(solution)/shard_map/ppermute | solution.py:25
  12.9 0.7 fusion.63
  13.7 1.3 %collective-permute-start.3 = (bf16[32,128]{1,0:T(8,128)(2,1)S(1)}, bf16[32,128]{1,0:T(8,128)(2,1)S(1)}, u32[]{:S(2)}, u32[]{:S(2)}) collective-permute-start(bf16[32,128]{1,0:T(8,128)(2,1)S(1)} %get-tuple-element.24), channel_id=1, source_target_pairs={{2,0},{3,1},{4,2},{5,3},{6,4},{7,5},{8,6},{9,7},{10,8},{11,9},{12,... | collective-permute-start | bytes 24584 | tf_op jit(solution)/shard_map/ppermute | solution.py:25
  14.9 4.0 %collective-permute-start.2 = (bf16[32,128]{1,0:T(8,128)(2,1)S(1)}, bf16[32,128]{1,0:T(8,128)(2,1)S(1)}, u32[]{:S(2)}, u32[]{:S(2)}) collective-permute-start(bf16[32,128]{1,0:T(8,128)(2,1)S(1)} %get-tuple-element.25), channel_id=1, source_target_pairs={{0,2},{1,3},{2,4},{3,5},{4,6},{5,7},{6,8},{7,9},{8,10},{9,11},{10,... | collective-permute-start | bytes 24584 | tf_op jit(solution)/shard_map/ppermute | solution.py:25
  19.0 1.0 reduce-window.9
  20.2 0.8 fusion.62
  21.0 0.6 convert_reduce_fusion
  21.6 0.6 dynamic_slice.14
  23.8 0.9 broadcast_multiply_fusion
  25.6 1.6 %pad_maximum_fusion.up_ref = bf16[128,1024]{1,0:T(8,128)(2,1)} fusion(bf16[128,512]{1,0:T(8,128)(2,1)} %param.36, bf16[128,512]{1,0:T(8,128)(2,1)S(1)} %broadcast_multiply_fusion), kind=kLoop, calls=%fused_computation.30 | loop fusion | flops 524288 | bytes 524288 | tf_op jit(solution)/shard_map/concatenate | solution.py:295
  27.4 0.7 broadcast_in_dim_reshape.7.ids_row
  28.1 0.8 broadcast_in_dim_reshape.8.ids_col
  28.9 0.9 copy.36
  29.7 0.9 copy.37
  30.7 0.5 slice.153
  31.2 0.5 slice.152
  31.7 1.4 %fusion.57 = s32[4]{0:T(128)S(1)} fusion(bf16[1]{0:T(256)(128)(2,1)} %bitcast.1, bf16[2]{0:T(256)(128)(2,1)S(1)} %subtract_convert_fusion, bf16[1]{0:T(256)(128)(2,1)} %bitcast, s32[]{:T(128)S(6)} %mul.68), kind=kLoop, calls=%fused_computation.100 | loop fusion | flops 40 | bytes 28 | tf_op jit(solution)/shard_map/add | solution.py:276
  33.2 0.7 constant_dynamic-update-slice_fusion.1
  34.3 0.8 fusion.19
  38.5 0.6 slice.173.single_ref
  39.1 0.8 convolution_convert_fusion.8.lr_ref
  39.9 42.5 %shard_map.193 = (bf16[64,128]{1,0:T(8,128)(2,1)}, bf16[8,384]{1,0:T(8,128)(2,1)}) custom-call(s32[256,1]{1,0:T(8,128)} %broadcast_in_dim_reshape.8.ids_col, s32[1,256]{1,0:T(1,128)} %broadcast_in_dim_reshape.7.ids_row, bf16[8,128]{1,0:T(8,128)(2,1)} %convolution_convert_fusion.8.lr_ref, bf16[8,384]{1,0:T(8,128)(2,1)} %slice.173.single_ref), custom_call_target="tpu_custom_call" | custom-call | tf_op jit(solution)/shard_map/pallas_call | solution.py:177
  82.5 1.3 %slice.147 = bf16[4,384]{1,0:T(4,128)(2,1)} slice(bf16[8,384]{1,0:T(8,128)(2,1)} %get-tuple-element.17), slice={[0:4], [0:384]} | slice | bytes 6144 | tf_op jit(solution)/shard_map/slice | solution.py:297
  83.7 0.8 copy.41
  84.6 0.6 slice_bitcast_fusion.right_ref
  85.2 1.0 fusion.13
  86.2 1.1 %copy.45.table_ref = bf16[64,32,128]{2,1,0:T(8,128)(2,1)} copy(bf16[64,32,128]{2,0,1:T(8,128)(2,1)S(1)} %fusion.13) | data formatting | bytes 1048576 | tf_op jit(solution)/shard_map/ai,abc->ibc/dot_general | solution.py:293
  87.3 0.9 fusion.10
  88.2 18.2 %shard_map.194 = bf16[64,128,128]{2,1,0:T(8,128)(2,1)} custom-call(bf16[64,128,128]{2,1,0:T(8,128)(2,1)} %pair_ref.1, bf16[64,32,128]{2,1,0:T(8,128)(2,1)} %copy.45.table_ref, bf16[128,32]{1,0:T(8,128)(2,1)} %slice_bitcast_fusion.right_ref, f32[1,128]{1,0:T(1,128)} %bitcast.28, bf16[128,1024]{1,0:T(8,128)(2,1)} %pad_maximum_fusion.up_ref, ...), custom_call_target="tpu_custom_call" | custom-call | tf_op jit(solution)/shard_map/pallas_call | solution.py:216
  (73 shorter events, 4.9 us)
Async XLA Ops:
  0.6 84.6 %copy-start = (bf16[32,32,128]{2,1,0:T(8,128)(2,1)S(1)}, bf16[32,32,128]{2,1,0:T(8,128)(2,1)}, u32[]{:S(2)}) copy-start(bf16[32,32,128]{2,1,0:T(8,128)(2,1)} %param.33) | copy-start | bytes 786436
  0.6 34.5 %copy-start.3 = (bf16[128,128]{1,0:T(8,128)(2,1)S(1)}, bf16[128,128]{1,0:T(8,128)(2,1)}, u32[]{:S(2)}) copy-start(bf16[128,128]{1,0:T(8,128)(2,1)} %param.24) | copy-start | bytes 98308
  0.7 34.7 %copy-start.4 = (bf16[128,128]{1,0:T(8,128)(2,1)S(1)}, bf16[128,128]{1,0:T(8,128)(2,1)}, u32[]{:S(2)}) copy-start(bf16[128,128]{1,0:T(8,128)(2,1)} %param.25) | copy-start | bytes 98308
  0.7 36.1 %copy-start.5 = (bf16[128,128]{1,0:T(8,128)(2,1)S(1)}, bf16[128,128]{1,0:T(8,128)(2,1)}, u32[]{:S(2)}) copy-start(bf16[128,128]{1,0:T(8,128)(2,1)} %param.26) | copy-start | bytes 98308
  2.3 28.4 %collective-permute-start.1 = (bf16[72,128]{1,0:T(8,128)(2,1)S(1)}, bf16[72,128]{1,0:T(8,128)(2,1)S(1)}, u32[]{:S(2)}, u32[]{:S(2)}) collective-permute-start(bf16[72,128]{1,0:T(8,128)(2,1)S(1)} %pad_maximum_fusion.1), channel_id=1, source_target_pairs={{1,0},{2,1},{3,2},{4,3},{5,4},{6,5},{7,6},{8,7},{9,8},{10,9},{11,1... | collective-permute-start | bytes 55304 | tf_op jit(solution)/shard_map/ppermute | solution.py:25
  11.0 20.2 %collective-permute-start = (bf16[72,128]{1,0:T(8,128)(2,1)S(1)}, bf16[72,128]{1,0:T(8,128)(2,1)S(1)}, u32[]{:S(2)}, u32[]{:S(2)}) collective-permute-start(bf16[72,128]{1,0:T(8,128)(2,1)S(1)} %pad_maximum_fusion.1), channel_id=1, source_target_pairs={{0,1},{1,2},{2,3},{3,4},{4,5},{5,6},{6,7},{7,8},{8,9},{9,10},{10,1... | collective-permute-start | bytes 55304 | tf_op jit(solution)/shard_map/ppermute | solution.py:25
  13.7 20.3 %collective-permute-start.3 = (bf16[32,128]{1,0:T(8,128)(2,1)S(1)}, bf16[32,128]{1,0:T(8,128)(2,1)S(1)}, u32[]{:S(2)}, u32[]{:S(2)}) collective-permute-start(bf16[32,128]{1,0:T(8,128)(2,1)S(1)} %get-tuple-element.24), channel_id=1, source_target_pairs={{2,0},{3,1},{4,2},{5,3},{6,4},{7,5},{8,6},{9,7},{10,8},{11,9},{12,... | collective-permute-start | bytes 24584 | tf_op jit(solution)/shard_map/ppermute | solution.py:25
  14.9 15.7 %collective-permute-start.2 = (bf16[32,128]{1,0:T(8,128)(2,1)S(1)}, bf16[32,128]{1,0:T(8,128)(2,1)S(1)}, u32[]{:S(2)}, u32[]{:S(2)}) collective-permute-start(bf16[32,128]{1,0:T(8,128)(2,1)S(1)} %get-tuple-element.25), channel_id=1, source_target_pairs={{0,2},{1,3},{2,4},{3,5},{4,6},{5,7},{6,8},{7,9},{8,10},{9,11},{10,... | collective-permute-start | bytes 24584 | tf_op jit(solution)/shard_map/ppermute | solution.py:25
  30.7 7.3 %copy-start.1 = (bf16[64,128]{1,0:T(8,128)(2,1)S(1)}, bf16[64,128]{1,0:T(8,128)(2,1)}, u32[]{:S(2)}) copy-start(bf16[64,128]{1,0:T(8,128)(2,1)} %param.20) | copy-start | bytes 49156
  30.7 7.3 %copy-start.7 = (bf16[128,128]{1,0:T(8,128)(2,1)S(1)}, bf16[128,128]{1,0:T(8,128)(2,1)}, u32[]{:S(2)}) copy-start(bf16[128,128]{1,0:T(8,128)(2,1)} %param.27) | copy-start | bytes 98308
  34.1 4.1 %copy-start.6 = (bf16[128,384]{1,0:T(8,128)(2,1)S(1)}, bf16[128,384]{1,0:T(8,128)(2,1)}, u32[]{:S(2)}) copy-start(bf16[128,384]{1,0:T(8,128)(2,1)} %param.28) | copy-start | bytes 294916
  37.3 50.1 %copy-start.2 = (bf16[384,128]{1,0:T(8,128)(2,1)S(1)}, bf16[384,128]{1,0:T(8,128)(2,1)}, u32[]{:S(2)}) copy-start(bf16[384,128]{1,0:T(8,128)(2,1)} %param.29) | copy-start | bytes 294916

commit v3 on v1

v3 whole, which is shorter than its diff:
```python
import functools

import jax
import jax.numpy as jnp
from jax import lax
from jax.experimental import pallas as pl
from jax.experimental.pallas import tpu as pltpu
from jax.sharding import PartitionSpec as P

MESH = pl.DeviceIdType.MESH
VMEM = pl.BlockSpec(memory_space=pltpu.VMEM)

HEADS = 4
QB = 32
KW = 128
FEWEST = 8
MOST = 24
EPSILON = 1e-05
BOTH = ("row", "col")


def layer_norm(values, gain):
    mean_value = jnp.mean(values, axis=-1, keepdims=True)
    centred = values - mean_value
    variance = jnp.mean(centred * centred, axis=-1, keepdims=True)
    return centred * lax.rsqrt(variance + EPSILON) * gain


def project(source, weight):
    return jnp.dot(source, weight, preferred_element_type=jnp.float32).astype(jnp.bfloat16)


def lanes(shape):
    return lax.broadcasted_iota(jnp.int32, shape, 1)


def lines(shape):
    return lax.broadcasted_iota(jnp.int32, shape, 0)


def onehot(condition):
    return jnp.where(condition, 1.0, 0.0).astype(jnp.bfloat16)


def dot(a, b):
    return jnp.dot(a, b, preferred_element_type=jnp.float32)


def each(low, high, act):
    def body(k, _):
        act(k)
        return 0
    lax.fori_loop(low, high, body, 0)


def front_kernel(rows, cols, own, feats, key_starts, counts, gain, wq, wk, wv, wo, wp, wb, wl, wr,
                 atom_out, ts_out, right_out, left_out,
                 off, offbuf, ext, lrow, comb, lbuf, cbuf, lall, call, lsend, lrecv, tsend, trecv, tsum,
                 hs, hr, s1, r1, s2, r2, s3, r3, s4, r4):
    row, col = lax.axis_index("row"), lax.axis_index("col")
    devices = rows * cols
    spot = row * cols + col
    atoms, width = feats.shape
    first = spot * atoms
    f32, b16 = jnp.float32, jnp.bfloat16

    def beside(distance):
        peer = lax.rem(spot + (distance + devices), devices)
        return (lax.div(peer, cols), lax.rem(peer, cols))

    def row_peer(k):
        return (lax.rem(row + k, rows), col)

    def col_peer(k):
        return (row, lax.rem(col + k, cols))

    barrier = pltpu.get_barrier_semaphore()

    def hail(target):
        pl.semaphore_signal(barrier, inc=1, device_id=target, device_id_type=MESH)

    each(1, rows, lambda k: hail(row_peer(k)))
    for distance in (1, -1, 2, -2):
        hail(beside(distance))
    each(1, cols, lambda k: hail(col_peer(k)))

    at = lines((16, width))
    plain = [key_starts[b] - (first + b * QB - KW // 2) for b in range(2)]
    off[...] = jnp.where(at == 0, plain[0], jnp.where(at == 1, plain[1], 0)).astype(f32).astype(b16)
    ext[96:160, :] = feats[...]

    tally = counts[...].astype(f32)
    tally16 = tally.astype(b16)
    within = dot(tally16, onehot(lines((128, 128)) <= lanes((128, 128))))
    whole = dot(tally16, jnp.ones((128, 128), b16))
    first_f = first.astype(f32)
    atom_f = lines((128, 128)).astype(f32) + (first_f - 32.0)
    carry = jnp.zeros((1, 128), f32)
    passed = jnp.zeros((128, 128), f32)
    before = jnp.zeros((1, 128), f32)
    after = jnp.zeros((1, 128), f32)
    for r in range(tally.shape[0]):
        end = within[r:r + 1, :] + carry
        begin = end - tally[r:r + 1, :]
        carry = carry + whole[r:r + 1, :]
        passed = passed + jnp.where(end <= atom_f, 1.0, 0.0)
        before = before + jnp.where(begin < first_f, 1.0, 0.0)
        after = after + jnp.where(begin < first_f + atoms, 1.0, 0.0)
    base = jnp.sum(before, axis=1, keepdims=True)
    held = jnp.sum(after, axis=1, keepdims=True) - base
    token = jnp.sum(passed, axis=1, keepdims=True) - base
    place = jnp.where(token == -1.0, 15.0, token)
    real = (atom_f >= 0.0) & (atom_f < float(atoms * devices))
    member_t = jnp.where((place == lanes((128, 128)).astype(f32)) & real, 1.0, 0.0)
    member = member_t.T[:16].astype(b16)

    pl.semaphore_wait(barrier, rows + cols + 2)
    halo = [(feats, ext.at[pl.ds(32, 64)], 1), (feats, ext.at[pl.ds(160, 64)], -1),
            (feats.at[pl.ds(32, 32)], ext.at[pl.ds(0, 32)], 2),
            (feats.at[pl.ds(0, 32)], ext.at[pl.ds(224, 32)], -2),
            (off, offbuf.at[0], 1), (off, offbuf.at[1], -1)]
    halo = [pltpu.make_async_remote_copy(
        src_ref=src, dst_ref=dst, send_sem=hs.at[n], recv_sem=hr.at[n],
        device_id=beside(distance), device_id_type=MESH) for n, (src, dst, distance) in enumerate(halo)]
    for copy in halo:
        copy.start()
    for copy in halo:
        copy.wait_recv()

    around = ext[...]
    normed = layer_norm(around.astype(f32), gain[...]).astype(b16)
    keys = dot(normed, wk[...]).astype(b16)
    values = dot(normed, wv[...]).astype(b16)
    queries = dot(normed[64:192], wq[...]).astype(b16)
    block = lines((128, 128)) // QB
    mine = off[...].astype(f32)
    offset = jnp.where(block == 0, offbuf[0].astype(f32)[1:2, :],
                       jnp.where(block == 1, mine[0:1, :],
                                 jnp.where(block == 2, mine[1:2, :], offbuf[1].astype(f32)[0:1, :])))
    offset = offset + (block * QB).astype(f32)
    spread_lane = lanes((128, 256)).astype(f32)
    from_start = spread_lane - jnp.concatenate([offset, offset], axis=1)
    key_atom = spread_lane + (first_f - 96.0)
    mask = ((from_start >= 0.0) & (from_start < float(KW)) & (key_atom >= 0.0)
            & (key_atom < float(atoms * devices)))
    exists = jnp.concatenate([real, real], axis=1)[:, :1]
    head = width // HEADS
    q_head, v_head = lanes((128, width)) // head, lanes((256, width)) // head
    attended = jnp.zeros((128, width), f32)
    for h in range(HEADS):
        query = jnp.where(q_head == h, queries.astype(f32), 0.0).astype(b16)
        value = jnp.where(v_head == h, values.astype(f32), 0.0).astype(b16)
        scores = lax.dot_general(query, keys, (((1,), (1,)), ((), ())),
                                 preferred_element_type=f32) * head ** (-0.5)
        raised = jnp.where(mask, jnp.exp(scores), 0.0)
        total = jnp.where(exists, jnp.sum(raised, axis=1, keepdims=True), 1.0)
        attended = attended + dot((raised / total).astype(b16), value)
    updated = (around[64:192].astype(f32) + dot(attended.astype(b16), wo[...])).astype(b16)
    feature = jnp.maximum(dot(updated, wp[...]), 0.0).astype(b16)
    number = jnp.maximum(dot(member, jnp.ones((128, 128), b16)), 1.0)
    wide = feature.shape[1]
    mean = dot(member, feature) / jnp.concatenate([number] * (wide // 128), axis=1)
    single = mean.astype(b16)
    left = dot(single, wl[...]).astype(b16)
    right = dot(single, wr[...]).astype(b16)
    opm = wl.shape[1]
    both = (dot(left, onehot(lanes((opm, 128)) == lines((opm, 128))))
            + dot(right, onehot(lanes((opm, 128)) == lines((opm, 128)) + opm)))
    slot = lines((16, 128)).astype(f32)
    ident = (slot + base).astype(jnp.int32)
    upper = jnp.where(slot < held, (ident >> 6).astype(f32), -1.0)
    lower = (ident & 63).astype(f32)
    both = jnp.where(lanes((16, 128)) == 64, upper, jnp.where(lanes((16, 128)) == 65, lower, both))
    lrow[...] = both[:8].astype(b16)
    comb[:, :wide] = mean[:8].astype(b16)
    comb[:, wide:] = both[:8].astype(b16)

    def push(src, buf, slot_at, send, recv, k, target):
        return pltpu.make_async_remote_copy(
            src_ref=src, dst_ref=buf.at[slot_at], send_sem=send.at[k], recv_sem=recv.at[slot_at],
            device_id=target, device_id_type=MESH)

    lr1 = lambda k, at: push(lrow, lbuf, at, s1, r1, k, row_peer(k))
    ts1 = lambda k, at: push(comb, cbuf, at, s2, r2, k, col_peer(k))
    lr2 = lambda k, at: push(lsend.at[lax.rem(col + k, cols)], lrecv, at, s3, r3, k, col_peer(k))
    ts2 = lambda k, at: push(tsend.at[lax.rem(row + k, rows)], trecv, at, s4, r4, k, row_peer(k))
    each(1, rows, lambda k: lr1(k, row).start())
    each(1, cols, lambda k: ts1(k, col).start())
    lbuf[row] = lrow[...]
    cbuf[col] = comb[...]

    back = jnp.concatenate([dot(single, wb[...]), jnp.zeros((112, width), f32)], axis=0).astype(b16)
    lifted = dot(member_t[32:96].astype(b16), back)
    atom_out[...] = (updated[32:96].astype(f32) + lifted).astype(b16)

    line = lines((rows * 16, 128))
    part, within_part = line // 16, line % 16
    want = (part * (own * cols) + col * own + within_part % 4).astype(f32)
    group = within_part // 4
    each(1, cols, lambda k: ts1(k, lax.rem(col + k, cols)).wait_recv())
    for c in range(cols):
        call[c * 8:(c + 1) * 8, :] = cbuf[c].astype(f32)
    turned = call[:, wide:].T
    same = want == turned[64:65, :] * 64.0 + turned[65:66, :]
    parts = jnp.zeros((rows * 16, 128), f32)
    for g in range(wide // 128):
        parts = parts + dot(onehot(same & (group == g)), call[:, g * 128:(g + 1) * 128].astype(b16))
    for r in range(rows):
        tsend[r] = parts[r * 16:(r + 1) * 16].astype(b16)
    each(1, rows, lambda k: ts2(k, row).start())
    trecv[row] = tsend[row]

    each(1, rows, lambda k: lr1(k, lax.rem(row + k, rows)).wait_recv())
    for r in range(rows):
        lall[r * 8:(r + 1) * 8, :] = lbuf[r].astype(f32)
    slots = lall[...]
    ident_col = slots[:, 64:65] * 64.0 + slots[:, 65:66]
    table = slots.T.astype(b16)
    lane_f = lanes((rows * 8, 128)).astype(f32)
    near = ident_col - (row * (own * cols)).astype(f32)
    left_t = dot(table[:opm], onehot(near == lane_f)).astype(b16)
    for c in range(cols):
        lsend[c, :opm] = dot(table[opm:2 * opm], onehot(ident_col - float(128 * c) == lane_f)).astype(b16)
        lsend[c, opm:] = left_t
    each(1, cols, lambda k: lr2(k, col).start())
    lrecv[col] = lsend[col]
    each(1, cols, lambda k: lr2(k, lax.rem(col + k, cols)).wait_recv())
    total = lrecv[0].astype(f32)
    for c in range(1, cols):
        total = total + lrecv[c].astype(f32)
    left_out[...] = total[opm:].astype(b16)
    right_out[...] = jnp.concatenate([total, total], axis=0).T[:, :opm].astype(b16)

    each(1, rows, lambda k: ts2(k, lax.rem(row + k, rows)).wait_recv())
    total = trecv[0].astype(f32)
    for r in range(1, rows):
        total = total + trecv[r].astype(f32)
    tsum[...] = total
    for g in range(wide // 128):
        ts_out[:, g * 128:(g + 1) * 128] = tsum[g * 4:(g + 1) * 4, :].astype(b16)

    for copy in halo:
        copy.wait_send()
    each(1, rows, lambda k: lr1(k, row).wait_send())
    each(1, cols, lambda k: ts1(k, col).wait_send())
    each(1, rows, lambda k: ts2(k, row).wait_send())
    each(1, cols, lambda k: lr2(k, col).wait_send())


def front(rows, cols, own, *args):
    atoms, width = args[0].shape
    wide, opm = args[9].shape[0], args[10].shape[1]
    kept = jnp.bfloat16
    dma = pltpu.SemaphoreType.DMA
    return pl.pallas_call(
        functools.partial(front_kernel, rows, cols, own),
        out_shape=(jax.ShapeDtypeStruct((atoms, width), kept), jax.ShapeDtypeStruct((own, wide), kept),
                   jax.ShapeDtypeStruct((128, opm), kept), jax.ShapeDtypeStruct((opm, 128), kept)),
        in_specs=[VMEM, pl.BlockSpec(memory_space=pltpu.SMEM)] + [VMEM] * 10,
        out_specs=(VMEM,) * 4,
        scratch_shapes=[
            pltpu.VMEM((16, width), kept),
            pltpu.VMEM((2, 16, width), kept),
            pltpu.VMEM((256, width), kept),
            pltpu.VMEM((8, 128), kept),
            pltpu.VMEM((8, wide + 128), kept),
            pltpu.VMEM((rows, 8, 128), kept),
            pltpu.VMEM((cols, 8, wide + 128), kept),
            pltpu.VMEM((rows * 8, 128), jnp.float32),
            pltpu.VMEM((cols * 8, wide + 128), jnp.float32),
            pltpu.VMEM((cols, 2 * opm, 128), kept),
            pltpu.VMEM((cols, 2 * opm, 128), kept),
            pltpu.VMEM((rows, 16, 128), kept),
            pltpu.VMEM((rows, 16, 128), kept),
            pltpu.VMEM((16, 128), jnp.float32),
            dma((6,)), dma((6,)), dma((rows,)), dma((rows,)), dma((cols,)), dma((cols,)),
            dma((cols,)), dma((cols,)), dma((rows,)), dma((rows,)),
        ],
        compiler_params=pltpu.CompilerParams(collective_id=0, has_side_effects=True),
    )(*args)


def pair_kernel(pair_ref, table_ref, right_ref, gain_ref, gate_ref, lift_ref, drop_ref, out_ref, up_ref):
    @pl.when(pl.program_id(0) == 0)
    def _():
        units = drop_ref.shape[0]
        up_ref[:, :units] = gate_ref[...] * 0.5
        up_ref[:, units:] = lift_ref[...]

    count, tokens, width = pair_ref.shape
    right = right_ref[...]
    outer = jnp.concatenate([
        jnp.dot(right, table_ref[i], preferred_element_type=jnp.float32) for i in range(count)], axis=0)
    summed = pair_ref[...].astype(jnp.float32).reshape(count * tokens, width) + outer
    normed = layer_norm(summed, gain_ref[...]).astype(jnp.bfloat16)
    raised = jnp.dot(normed, up_ref[...], preferred_element_type=jnp.float32)
    units = drop_ref.shape[0]
    half = raised[:, :units]
    hidden = ((half + half * jnp.tanh(half)) * raised[:, units:]).astype(jnp.bfloat16)
    total = summed + jnp.dot(hidden, drop_ref[...], preferred_element_type=jnp.float32)
    out_ref[...] = total.astype(jnp.bfloat16).reshape(count, tokens, width)


def pair_update(pair_state, table, right, gain, gate, lift, drop):
    rows, tokens, width = pair_state.shape
    step = 4
    whole = lambda a: pl.BlockSpec(a.shape, lambda i: (0,) * a.ndim)
    tile = pl.BlockSpec((step, tokens, width), lambda i: (i, 0, 0))
    return pl.pallas_call(
        pair_kernel,
        grid=(rows // step,),
        out_shape=jax.ShapeDtypeStruct(pair_state.shape, pair_state.dtype),
        in_specs=[tile, pl.BlockSpec((step,) + table.shape[1:], lambda i: (i, 0, 0)), whole(right),
                  whole(gain), whole(gate), whole(lift), whole(drop)],
        out_specs=tile,
        scratch_shapes=[pltpu.VMEM((width, 2 * drop.shape[0]), jnp.bfloat16)],
    )(pair_state, table, right, gain, gate, lift, drop)


def per_device(
    atom_feats,
    key_starts,
    atom_counts,
    atom_gain,
    w_query,
    w_key,
    w_value,
    w_out,
    w_pool,
    w_back,
    pair_state,
    w_left,
    w_right,
    w_outer,
    pair_gain,
    w_gate,
    w_lift,
    w_drop,
):
    rows, cols = lax.axis_size("row"), lax.axis_size("col")
    own = atom_counts.shape[0] // (rows * cols)
    atom_out, token_single, right, left = front(
        rows, cols, own, atom_feats, key_starts, atom_counts.reshape(-1, 128), atom_gain[None, :],
        w_query, w_key, w_value, w_out, w_pool, w_back, w_left, w_right)
    table = jnp.einsum("ai,abc->ibc", left[:, :pair_state.shape[0]], w_outer,
                       preferred_element_type=jnp.float32).astype(jnp.bfloat16)
    pair_out = pair_update(pair_state, table, right, pair_gain[None, :], w_gate, w_lift, w_drop)
    return atom_out, token_single, pair_out


def solution(mesh):
    whole = P(BOTH, None)
    in_specs = (whole, P(BOTH)) + (P(),) * 8 + (P("row", "col", None),) + (P(),) * 7
    out_specs = (whole, whole, P("row", "col", None))
    return jax.shard_map(
        per_device, mesh=mesh, in_specs=in_specs, out_specs=out_specs, check_vma=False
    )
```

time: 334 us -> 68.9 us (0.21)
  the two profiles are of different devices: /device:TPU:2 before, /device:TPU:1 now
where the time goes in v3:
time: 68.9 us; the launch traced here: 68.2 us
  Pallas kernels  61.2 us (89%)
  local copies, waits for them, and re-layouts  5.32 us (8%)
  matrix products  1.02 us (1%)
    pallas_call x1, Pallas kernels, front(): pl.pallas_call(functools.partial(front_kernel, rows, cols, own), out_shap...  42.8 us
    pallas_call x1, Pallas kernels, pair_update(): pl.pallas_call(pair_kernel, grid=(rows // step,), out_shape=jax.ShapeDtyp...  18.3 us
    unnamed x10, local copies, waits for them, and re-layouts  4.19 us

profile of v3, /device:TPU:1, one launch (start us, length us, event | category | flops | bytes accessed | tf_op | source)
XLA Modules:
  0.0 68.2 jit_solution(10816496172844331210)
XLA Ops:
  0.6 0.0 copy-start
  0.6 1.5 %copy.21.wl = bf16[384,32]{1,0:T(8,128)(2,1)} copy(bf16[384,32]{0,1:T(8,128)(2,1)} %param.29) | data formatting | bytes 49152 | tf_op args[11]
  2.2 1.5 %copy.22.wr = bf16[384,32]{1,0:T(8,128)(2,1)} copy(bf16[384,32]{0,1:T(8,128)(2,1)} %param.30) | data formatting | bytes 49152 | tf_op args[12]
  3.6 42.8 %shard_map.193 = (bf16[64,128]{1,0:T(8,128)(2,1)}, bf16[4,384]{1,0:T(4,128)(2,1)}, bf16[128,32]{1,0:T(8,128)(2,1)}, bf16[32,128]{1,0:T(8,128)(2,1)}) custom-call(bf16[64,128]{1,0:T(8,128)(2,1)} %feats.1, s32[2]{0:T(128)} %key_starts.1, s32[16,128]{1,0:T(8,128)} %bitcast.6, f32[1,128]{1,0:T(1,128)} %bitcast.7, bf16[128,128]{1,0:T(8,128)(2,1)} %wq.1, ...), custom_call_target="tpu_custom_call" | custom-call | tf_op jit(solution)/shard_map/pallas_call | solution.py:255
  46.5 0.0 copy-done
  46.5 1.0 %fusion = bf16[64,32,128]{2,0,1:T(8,128)(2,1)S(1)} fusion(bf16[32,32,128]{2,1,0:T(8,128)(2,1)S(1)} %copy-done, bf16[32,128]{1,0:T(8,128)(2,1)} %get-tuple-element.9), kind=kOutput, calls=%fused_computation.1 | convolution fusion | flops 16777216 | bytes 794624 | tf_op jit(solution)/shard_map/ai,abc->ibc/dot_general | solution.py:345
  47.5 1.1 %copy.28.table_ref = bf16[64,32,128]{2,1,0:T(8,128)(2,1)} copy(bf16[64,32,128]{2,0,1:T(8,128)(2,1)S(1)} %fusion) | data formatting | bytes 1048576 | tf_op jit(solution)/shard_map/ai,abc->ibc/dot_general | solution.py:345
  48.7 0.0 copy-start.1
  48.7 0.0 copy-start.2
  48.7 18.3 %shard_map.194 = bf16[64,128,128]{2,1,0:T(8,128)(2,1)} custom-call(bf16[64,128,128]{2,1,0:T(8,128)(2,1)} %pair_ref.1, bf16[64,32,128]{2,1,0:T(8,128)(2,1)} %copy.28.table_ref, bf16[128,32]{1,0:T(8,128)(2,1)} %get-tuple-element.10.right_ref, f32[1,128]{1,0:T(1,128)} %bitcast.8, bf16[128,512]{1,0:T(8,128)(2,1)} %gate_ref.1, bf16[128,512]{1,0:T(8,128)(2,1)} %lift_ref.1, ...), custom_call_target="tpu_custom_call" | custom-call | tf_op jit(solution)/shard_map/pallas_call | solution.py:309
  67.0 0.0 copy-done.1
  67.0 0.6 copy.31
  67.6 0.0 copy-done.2
  67.6 0.6 copy.32
Async XLA Ops:
  0.6 45.9 %copy-start = (bf16[32,32,128]{2,1,0:T(8,128)(2,1)S(1)}, bf16[32,32,128]{2,1,0:T(8,128)(2,1)}, u32[]{:S(2)}) copy-start(bf16[32,32,128]{2,1,0:T(8,128)(2,1)} %param.31) | copy-start | bytes 786436
  48.7 18.3 %copy-start.1 = (bf16[64,128]{1,0:T(8,128)(2,1)S(1)}, bf16[64,128]{1,0:T(8,128)(2,1)}, u32[]{:S(2)}) copy-start(bf16[64,128]{1,0:T(8,128)(2,1)} %get-tuple-element.14) | copy-start | bytes 49156
  48.7 18.9 %copy-start.2 = (bf16[4,384]{1,0:T(4,128)(2,1)S(1)}, bf16[4,384]{1,0:T(4,128)(2,1)}, u32[]{:S(2)}) copy-start(bf16[4,384]{1,0:T(4,128)(2,1)} %get-tuple-element.15) | copy-start | bytes 9220

commit v4 on v3

--- a/solution.py
+++ b/solution.py
@@ -161,9 +161,10 @@
     wide = feature.shape[1]
     mean = dot(member, feature) / jnp.concatenate([number] * (wide // 128), axis=1)
     single = mean.astype(b16)
-    left = dot(single, wl[...]).astype(b16)
-    right = dot(single, wr[...]).astype(b16)
-    opm = wl.shape[1]
+    flat = (((1,), (1,)), ((), ()))
+    left = lax.dot_general(single, wl[...], flat, preferred_element_type=f32).astype(b16)
+    right = lax.dot_general(single, wr[...], flat, preferred_element_type=f32).astype(b16)
+    opm = wl.shape[0]
     both = (dot(left, onehot(lanes((opm, 128)) == lines((opm, 128))))
             + dot(right, onehot(lanes((opm, 128)) == lines((opm, 128)) + opm)))
     slot = lines((16, 128)).astype(f32)
@@ -249,7 +250,7 @@
 
 def front(rows, cols, own, *args):
     atoms, width = args[0].shape
-    wide, opm = args[9].shape[0], args[10].shape[1]
+    opm, wide = args[10].shape
     kept = jnp.bfloat16
     dma = pltpu.SemaphoreType.DMA
     return pl.pallas_call(
@@ -280,12 +281,15 @@
     )(*args)
 
 
-def pair_kernel(pair_ref, table_ref, right_ref, gain_ref, gate_ref, lift_ref, drop_ref, out_ref, up_ref):
+def pair_kernel(pair_ref, table_ref, right_ref, gain_ref, gate_ref, lift_ref, drop_ref,
+                atom_ref, token_ref, out_ref, atom_out, token_out, up_ref):
     @pl.when(pl.program_id(0) == 0)
     def _():
         units = drop_ref.shape[0]
         up_ref[:, :units] = gate_ref[...] * 0.5
         up_ref[:, units:] = lift_ref[...]
+        atom_out[...] = atom_ref[...]
+        token_out[...] = token_ref[...]
 
     count, tokens, width = pair_ref.shape
     right = right_ref[...]
@@ -301,20 +305,20 @@
     out_ref[...] = total.astype(jnp.bfloat16).reshape(count, tokens, width)
 
 
-def pair_update(pair_state, table, right, gain, gate, lift, drop):
+def pair_update(pair_state, table, right, gain, gate, lift, drop, atom, token):
     rows, tokens, width = pair_state.shape
-    step = 4
+    step = 16
     whole = lambda a: pl.BlockSpec(a.shape, lambda i: (0,) * a.ndim)
     tile = pl.BlockSpec((step, tokens, width), lambda i: (i, 0, 0))
     return pl.pallas_call(
         pair_kernel,
         grid=(rows // step,),
-        out_shape=jax.ShapeDtypeStruct(pair_state.shape, pair_state.dtype),
+        out_shape=tuple(jax.ShapeDtypeStruct(a.shape, a.dtype) for a in (pair_state, atom, token)),
         in_specs=[tile, pl.BlockSpec((step,) + table.shape[1:], lambda i: (i, 0, 0)), whole(right),
-                  whole(gain), whole(gate), whole(lift), whole(drop)],
-        out_specs=tile,
+                  whole(gain), whole(gate), whole(lift), whole(drop), whole(atom), whole(token)],
+        out_specs=(tile, whole(atom), whole(token)),
         scratch_shapes=[pltpu.VMEM((width, 2 * drop.shape[0]), jnp.bfloat16)],
-    )(pair_state, table, right, gain, gate, lift, drop)
+    )(pair_state, table, right, gain, gate, lift, drop, atom, token)
 
 
 def per_device(
@@ -341,10 +345,11 @@
     own = atom_counts.shape[0] // (rows * cols)
     atom_out, token_single, right, left = front(
         rows, cols, own, atom_feats, key_starts, atom_counts.reshape(-1, 128), atom_gain[None, :],
-        w_query, w_key, w_value, w_out, w_pool, w_back, w_left, w_right)
+        w_query, w_key, w_value, w_out, w_pool, w_back, w_left.T, w_right.T)
     table = jnp.einsum("ai,abc->ibc", left[:, :pair_state.shape[0]], w_outer,
                        preferred_element_type=jnp.float32).astype(jnp.bfloat16)
-    pair_out = pair_update(pair_state, table, right, pair_gain[None, :], w_gate, w_lift, w_drop)
+    pair_out, atom_out, token_single = pair_update(
+        pair_state, table, right, pair_gain[None, :], w_gate, w_lift, w_drop, atom_out, token_single)
     return atom_out, token_single, pair_out
 
 

time: 68.9 us -> 59.3 us (0.86)
  Pallas kernels: 61.2 us -> 56 us
  local copies, waits for them, and re-layouts: 5.32 us -> 1.14 us
    pallas_call x1, Pallas kernels: 18.3 us -> 13.1 us  [pair_update(): pl.pallas_call(pair_kernel, grid=(rows // step,), out_shape=tuple((jax.Sh...]
    unnamed x10 -> x2, local copies, waits for them, and re-layouts: 4.19 us -> 0.01 us
where the time goes in v4:
time: 59.3 us; the launch traced here: 58.8 us
  Pallas kernels  56 us (94%)
  local copies, waits for them, and re-layouts  1.14 us (2%)
  matrix products  1.02 us (2%)
  between operations  0.67 us (1%)
    pallas_call x1, Pallas kernels, front(): pl.pallas_call(functools.partial(front_kernel, rows, cols, own), out_shap...  42.9 us
    pallas_call x1, Pallas kernels, pair_update(): pl.pallas_call(pair_kernel, grid=(rows // step,), out_shape=tuple((jax.Sh...  13.1 us

profile of v4, /device:TPU:1, one launch (start us, length us, event | category | flops | bytes accessed | tf_op | source)
XLA Modules:
  0.0 58.8 jit_solution(1087644125258656728)
XLA Ops:
  0.6 0.0 copy-start
  0.7 42.9 %shard_map.193 = (bf16[64,128]{1,0:T(8,128)(2,1)}, bf16[4,384]{1,0:T(4,128)(2,1)}, bf16[128,32]{1,0:T(8,128)(2,1)}, bf16[32,128]{1,0:T(8,128)(2,1)}) custom-call(bf16[64,128]{1,0:T(8,128)(2,1)} %feats.1, s32[2]{0:T(128)} %key_starts.1, s32[16,128]{1,0:T(8,128)} %bitcast.10, f32[1,128]{1,0:T(1,128)} %bitcast.11, bf16[128,128]{1,0:T(8,128)(2,1)} %wq.1, ...), custom_call_target="tpu_custom_call" | custom-call | tf_op jit(solution)/shard_map/pallas_call | solution.py:256
  43.5 0.0 copy-done
  43.5 1.0 %fusion = bf16[64,32,128]{2,0,1:T(8,128)(2,1)S(1)} fusion(bf16[32,32,128]{2,1,0:T(8,128)(2,1)S(1)} %copy-done, bf16[32,128]{1,0:T(8,128)(2,1)} %get-tuple-element.10), kind=kOutput, calls=%fused_computation.1 | convolution fusion | flops 16777216 | bytes 794624 | tf_op jit(solution)/shard_map/ai,abc->ibc/dot_general | solution.py:349
  44.6 1.1 %copy.26.table_ref = bf16[64,32,128]{2,1,0:T(8,128)(2,1)} copy(bf16[64,32,128]{2,0,1:T(8,128)(2,1)S(1)} %fusion) | data formatting | bytes 1048576 | tf_op jit(solution)/shard_map/ai,abc->ibc/dot_general | solution.py:349
  45.7 13.1 %shard_map.194 = (bf16[64,128,128]{2,1,0:T(8,128)(2,1)}, bf16[64,128]{1,0:T(8,128)(2,1)}, bf16[4,384]{1,0:T(4,128)(2,1)}) custom-call(bf16[64,128,128]{2,1,0:T(8,128)(2,1)} %pair_ref.1, bf16[64,32,128]{2,1,0:T(8,128)(2,1)} %copy.26.table_ref, bf16[128,32]{1,0:T(8,128)(2,1)} %get-tuple-element.11.right_ref, f32[1,128]{1,0:T(1,128)} %bitcast.12, ...), custom_call_target="tpu_custom_call" | custom-call | tf_op jit(solution)/shard_map/pallas_call | solution.py:313
Async XLA Ops:
  0.6 42.9 %copy-start = (bf16[32,32,128]{2,1,0:T(8,128)(2,1)S(1)}, bf16[32,32,128]{2,1,0:T(8,128)(2,1)}, u32[]{:S(2)}) copy-start(bf16[32,32,128]{2,1,0:T(8,128)(2,1)} %param.31) | copy-start | bytes 786436

commit v5 on v4

--- a/solution.py
+++ b/solution.py
@@ -220,10 +220,18 @@
     lane_f = lanes((rows * 8, 128)).astype(f32)
     near = ident_col - (row * (own * cols)).astype(f32)
     left_t = dot(table[:opm], onehot(near == lane_f)).astype(b16)
+
+    def forward(c):
+        @pl.when(col != c)
+        def _():
+            lr2(lax.rem(c - col + cols, cols), col).start()
+
     for c in range(cols):
         lsend[c, :opm] = dot(table[opm:2 * opm], onehot(ident_col - float(128 * c) == lane_f)).astype(b16)
         lsend[c, opm:] = left_t
-    each(1, cols, lambda k: lr2(k, col).start())
+        if c > 0:
+            forward(c - 1)
+    forward(cols - 1)
     lrecv[col] = lsend[col]
     each(1, cols, lambda k: lr2(k, lax.rem(col + k, cols)).wait_recv())
     total = lrecv[0].astype(f32)
@@ -307,7 +315,7 @@
 
 def pair_update(pair_state, table, right, gain, gate, lift, drop, atom, token):
     rows, tokens, width = pair_state.shape
-    step = 16
+    step = 32
     whole = lambda a: pl.BlockSpec(a.shape, lambda i: (0,) * a.ndim)
     tile = pl.BlockSpec((step, tokens, width), lambda i: (i, 0, 0))
     return pl.pallas_call(

time: 59.3 us -> 58.8 us (level)
  Pallas kernels: 56 us -> 54.9 us
    pallas_call x1, Pallas kernels: 13.1 us -> 12.5 us  [pair_update(): pl.pallas_call(pair_kernel, grid=(rows // step,), out_shape=tuple((jax.Sh...]
where the time goes in v5:
time: 58.8 us; the launch traced here: 57.8 us
  Pallas kernels  54.9 us (93%)
  local copies, waits for them, and re-layouts  1.14 us (2%)
  matrix products  1.01 us (2%)
  between operations  0.67 us (1%)
    pallas_call x1, Pallas kernels, front(): pl.pallas_call(functools.partial(front_kernel, rows, cols, own), out_shap...  42.4 us
    pallas_call x1, Pallas kernels, pair_update(): pl.pallas_call(pair_kernel, grid=(rows // step,), out_shape=tuple((jax.Sh...  12.5 us

profile of v5, /device:TPU:1, one launch (start us, length us, event | category | flops | bytes accessed | tf_op | source)
XLA Modules:
  0.0 57.8 jit_solution(2260682498484762214)
XLA Ops:
  0.6 0.0 copy-start
  0.7 42.4 %shard_map.193 = (bf16[64,128]{1,0:T(8,128)(2,1)}, bf16[4,384]{1,0:T(4,128)(2,1)}, bf16[128,32]{1,0:T(8,128)(2,1)}, bf16[32,128]{1,0:T(8,128)(2,1)}) custom-call(bf16[64,128]{1,0:T(8,128)(2,1)} %feats.1, s32[2]{0:T(128)} %key_starts.1, s32[16,128]{1,0:T(8,128)} %bitcast.10, f32[1,128]{1,0:T(1,128)} %bitcast.11, bf16[128,128]{1,0:T(8,128)(2,1)} %wq.1, ...), custom_call_target="tpu_custom_call" | custom-call | tf_op jit(solution)/shard_map/pallas_call | solution.py:264
  43.1 0.0 copy-done
  43.1 1.0 %fusion = bf16[64,32,128]{2,0,1:T(8,128)(2,1)S(1)} fusion(bf16[32,32,128]{2,1,0:T(8,128)(2,1)S(1)} %copy-done, bf16[32,128]{1,0:T(8,128)(2,1)} %get-tuple-element.10), kind=kOutput, calls=%fused_computation.1 | convolution fusion | flops 16777216 | bytes 794624 | tf_op jit(solution)/shard_map/ai,abc->ibc/dot_general | solution.py:357
  44.1 1.1 %copy.26.table_ref = bf16[64,32,128]{2,1,0:T(8,128)(2,1)} copy(bf16[64,32,128]{2,0,1:T(8,128)(2,1)S(1)} %fusion) | data formatting | bytes 1048576 | tf_op jit(solution)/shard_map/ai,abc->ibc/dot_general | solution.py:357
  45.2 12.5 %shard_map.194 = (bf16[64,128,128]{2,1,0:T(8,128)(2,1)}, bf16[64,128]{1,0:T(8,128)(2,1)}, bf16[4,384]{1,0:T(4,128)(2,1)}) custom-call(bf16[64,128,128]{2,1,0:T(8,128)(2,1)} %pair_ref.1, bf16[64,32,128]{2,1,0:T(8,128)(2,1)} %copy.26.table_ref, bf16[128,32]{1,0:T(8,128)(2,1)} %get-tuple-element.11.right_ref, f32[1,128]{1,0:T(1,128)} %bitcast.12, ...), custom_call_target="tpu_custom_call" | custom-call | tf_op jit(solution)/shard_map/pallas_call | solution.py:321
Async XLA Ops:
  0.6 42.4 %copy-start = (bf16[32,32,128]{2,1,0:T(8,128)(2,1)S(1)}, bf16[32,32,128]{2,1,0:T(8,128)(2,1)}, u32[]{:S(2)}) copy-start(bf16[32,32,128]{2,1,0:T(8,128)(2,1)} %param.31) | copy-start | bytes 786436
